TPU v7x, 32 devices: a whole 2x2x4 slice. The times are simulated.
32 devices in a mesh: ctx: 8 (over z, y), head: 4 (over x, core).
Axes of the slice: x: 2, y: 2, z: 4, core: 2. Of those that a mesh axis runs over, the one named last changes fastest.
Arguments:
- query_act: bfloat16 [2048, 2048], P('ctx', 'head'), may hold values from -5 to 5
- key_act: bfloat16 [2048, 2048], P('ctx', 'head'), may hold values from -5 to 5
- value_act: bfloat16 [2048, 2048], P('ctx', 'head'), may hold values from -6 to 6
- out_weight: bfloat16 [2048, 2048], P('head'), may hold values from -0.125 to 0.125
- cotangent: bfloat16 [2048, 2048], P('ctx', 'head'), may hold values from -6 to 6
- butterfly_cols: int32 [16, 3], replicated, may hold values from 0 to 15, as said below
- global_cols: int32 [256], replicated, may hold values from 0 to 2047, as said below
Outputs:
- layer_out: bfloat16 [2048, 2048], P('ctx', 'head')
- query_grad: bfloat16 [2048, 2048], P('ctx', 'head')
- key_grad: bfloat16 [2048, 2048], P('ctx', 'head')
- value_grad: bfloat16 [2048, 2048], P('ctx', 'head')
Inputs may be any that keep to these rules, and one draw needn't show every extreme that they name: `butterfly_cols`: entry [i, l] names one of the 2 blocks with index in the group (i // 2) xor 2**l, groups being runs of 2 consecutive block indices. `global_cols`: the positions are distinct.
All inputs are finite; a program needn't handle non-finite values.
Results may differ from a plain program's by a relative error of at most 0.0068.
Values may be sent and summed in bfloat16 or wider, within the bound.
No kernel may reach another device: no remote copies, remote signals or barrier semaphores. Data moves between devices by JAX's collectives and lax.ppermute only.
A program may use at most 64 MiB of HBM per device.

v0:
```python
import functools
import math

import jax
import jax.numpy as jnp
from jax import lax
from jax.experimental import pallas as pl
from jax.experimental.pallas import tpu as pltpu
from jax.sharding import PartitionSpec as P


HEAD_SIZE = 128
BLOCK = 128
STAT_ROWS = 8
KERNEL_VMEM = 16 * 2**20


FACTOR = 1.0 / math.sqrt(HEAD_SIZE)
NT = (((1,), (1,)), ((), ()))
TN = (((0,), (0,)), ((), ()))
F32 = jnp.float32
BF16 = jnp.bfloat16


def swap(shard, axis, mask):
    return lax.ppermute(shard, axis, [(i, i ^ mask) for i in range(lax.axis_size(axis))])


def call(kernel, out_shape, *operands, scalars=0, scratch=()):
    in_specs = [pl.BlockSpec(memory_space=pltpu.SMEM)] * scalars
    in_specs += [pl.BlockSpec(memory_space=pltpu.VMEM)] * (len(operands) - scalars)
    outs = [pl.BlockSpec(memory_space=pltpu.VMEM)] * len(out_shape)
    placed = [pltpu.with_memory_space_constraint(o, pltpu.VMEM) for o in operands[scalars:]]
    return pl.pallas_call(
        kernel,
        in_specs=in_specs,
        out_specs=outs,
        out_shape=out_shape,
        scratch_shapes=scratch,
        compiler_params=pltpu.CompilerParams(vmem_limit_bytes=KERNEL_VMEM),
    )(*operands[:scalars], *placed)


def like(shape, dtype=jnp.bfloat16):
    return pltpu.VMEM(shape, dtype)


def dot(a, b, dims=(((1,), (0,)), ((), ()))):
    return lax.dot_general(a, b, dims, preferred_element_type=F32)


def block_at(index):
    return pl.ds(pl.multiple_of(index * BLOCK, BLOCK), BLOCK)


def columns_of(head):
    return pl.ds(pl.multiple_of(head * HEAD_SIZE, HEAD_SIZE), HEAD_SIZE)


def grad_kernel(weight_ref, query, *refs):
    pieces, (out_ref, pair_ref) = refs[:-2], refs[-2:]
    rows = query.shape[0]
    width = pieces[0].shape[1]
    mine = lax.axis_index("head")
    total = None
    for m, piece in enumerate(pieces):
        start = pl.multiple_of(jnp.bitwise_xor(mine, m) * width, width)
        part = dot(piece[...], weight_ref[:, pl.ds(start, width)], NT)
        total = part if total is None else total + part
    out_ref[...] = total.astype(BF16)
    pair_ref[:rows, :] = query[...]
    pair_ref[rows:, :] = total.astype(BF16)


def project_kernel(att_ref, weight_ref, *outs):
    width = outs[0].shape[1]
    mine = lax.axis_index("head")
    for m, out in enumerate(outs):
        start = pl.multiple_of(jnp.bitwise_xor(mine, m) * width, width)
        out[...] = dot(att_ref[...], weight_ref[:, pl.ds(start, width)]).astype(out.dtype)


def hot_kernel(masks, groups, cols_ref, scatter_ref, *outs):
    rows, slots = scatter_ref.shape
    device = lax.axis_index("ctx")
    row_ids = lax.broadcasted_iota(jnp.int32, (rows, slots), 0)

    def local(mask):
        return cols_ref[...] - jnp.bitwise_xor(device, mask) * rows

    for mask, out in zip(masks, outs):
        chosen = (row_ids == local(mask)).astype(F32)
        if mask == 0:
            scatter_ref[...] = chosen.astype(BF16)
        out[...] = chosen.T.astype(BF16)
    for group, out in zip(groups, outs[len(masks) :]):
        owned = 0.0
        for mask in group:
            at = jnp.broadcast_to(local(mask), (out.shape[1], slots))
            owned = owned + jnp.logical_and(at >= 0, at < rows).astype(F32)
        out[...] = owned.T


def select_kernel(count, *refs):
    total = dot(refs[0][...], refs[count][...])
    for select, source in zip(refs[1:count], refs[count + 1 : -1]):
        total = total + dot(select[...], source[...])
    refs[-1][...] = total.astype(BF16)


def select_globals(selects, sources):
    shape = like((selects[0].shape[0], sources[0].shape[1]))
    kernel = functools.partial(select_kernel, len(selects))
    return call(kernel, [shape], *selects, *sources)[0]


def merged(parts, owned, at):
    total = parts[0][:, at].astype(F32)
    for part, mask in zip(parts[1:], owned):
        total = total + mask[...] * part[:, at].astype(F32)
    return total.astype(BF16)


def merge_kernel(have, got, owned, out):
    for start in range(0, out.shape[1], HEAD_SIZE):
        part = pl.ds(start, HEAD_SIZE)
        out[:, part] = merged((have, got), (owned,), part)


def merge(have, got, owned):
    return call(merge_kernel, [like(have.shape)], have, got, owned)[0]


def near_at(strides, device, blocks, i, cols_ref, own, far, part):
    picked = [
        far[s][
            block_at(cols_ref[s, device * blocks + i] - jnp.bitwise_xor(device, 1 << s) * blocks),
            part,
        ]
        for s in range(strides)
    ]
    return jnp.concatenate([own[pl.ds(i * BLOCK, BLOCK), part]] + picked, 0)


def put_columns(ref, rows, head, columns, step=1, width=STAT_ROWS):
    held = ref[rows, :]
    lane = lax.broadcasted_iota(jnp.int32, held.shape, 1)
    for place, column in enumerate(columns):
        held = jnp.where(lane == head * width + place * step, column, held)
    ref[rows, :] = held


def take_column(ref, rows, head, place):
    held = ref[rows, :]
    lane = lax.broadcasted_iota(jnp.int32, held.shape, 1)
    return jnp.sum(jnp.where(lane == head * STAT_ROWS + place, held, 0.0), axis=1, keepdims=True)


NOTES = 7


def thirds(column):
    high = column.astype(BF16).astype(F32)
    middle = (column - high).astype(BF16).astype(F32)
    return high, middle, column - high - middle


def note_lines(rows, width):
    groups = width // rows
    lines = -(-NOTES * (width // HEAD_SIZE) // groups)
    return groups, -(-lines // 16) * 16


def read_notes(message, stats, rows, heads):
    _, lines = note_lines(rows, message.shape[1])
    held = message[message.shape[0] - lines :, :].astype(F32)

    def line(place, head):
        group, at = divmod(place * heads + head, lines)
        return held[at : at + 1, group * rows : (group + 1) * rows]

    for head in range(heads):
        for place, parts in enumerate(((0,), (1, 2, 3), (4, 5, 6))):
            at = head * STAT_ROWS + place
            stats[at : at + 1, :] = sum(line(part, head) for part in parts)


def near_kernel(strides, parts, cols_ref, query, grad, *refs):
    own_key, own_value = refs[:2]
    far_keys, far_values = refs[2 : 2 + strides], refs[2 + strides : 2 + 2 * strides]
    globs, owned = refs[2 + 2 * strides :][:parts], refs[2 + 2 * strides + parts : -6]
    weight_out, prob_out, glob_out, term_out, key_out, stats = refs[-6:]
    blocks, heads = query.shape[0] // BLOCK, query.shape[1] // HEAD_SIZE
    near, slots = (strides + 1) * BLOCK, key_out.shape[0]
    device = lax.axis_index("ctx")

    def one_head(head, _):
        part = columns_of(head)
        wide = pl.ds(pl.multiple_of(head * near, near), near)
        glob = pl.ds(pl.multiple_of(head * slots, slots), slots)
        glob_key = merged(globs, owned, part)
        key_out[:, part] = glob_key
        rounded = []
        for i in range(blocks):
            rows = pl.ds(i * BLOCK, BLOCK)
            keys = near_at(strides, device, blocks, i, cols_ref, own_key, far_keys, part)
            values = near_at(strides, device, blocks, i, cols_ref, own_value, far_values, part)
            scores = dot(query[rows, part], jnp.concatenate([keys, glob_key], 0), NT) * FACTOR
            prob_grad = dot(grad[rows, part], values, NT)
            top = jnp.max(scores, axis=1, keepdims=True)
            top = top.astype(BF16).astype(F32)
            exponent = jnp.exp(scores - top)
            scale = 1.0 / jnp.sum(exponent, axis=1, keepdims=True)
            weights = exponent * scale
            weight_out[rows, wide] = weights[:, :near]
            prob_out[rows, wide] = prob_grad
            glob_out[rows, glob] = weights[:, near:]
            rounded.append(weights[:, near:].astype(BF16))
            delta = jnp.sum(weights[:, :near] * prob_grad, axis=1, keepdims=True)
            put_columns(stats, rows, head, (top, scale, delta))
        term_out[:, part] = dot(jnp.concatenate(rounded, 0), grad[:, part], TN)

    lax.fori_loop(0, heads, one_head, None, unroll=2)


def glob_kernel(parts, query, grad, near_stats, weights_in, value_term, *refs):
    values_in, owned = refs[:parts], refs[parts : 2 * parts - 1]
    keep_out, send_out, delta_out, score_out, value_out, stats = refs[2 * parts - 1 :]
    heads, slots = query.shape[1] // HEAD_SIZE, value_out.shape[0]
    odd = jnp.bitwise_and(lax.axis_index("ctx"), 1) == 1
    every = pl.ds(0, query.shape[0])

    def one_head(head, _):
        part = columns_of(head)
        glob = pl.ds(pl.multiple_of(head * slots, slots), slots)
        values = merged(values_in, owned, part)
        value_out[:, part] = values
        prob_grad = dot(grad[:, part], values, NT)
        top, scale, near_delta = (take_column(near_stats, every, head, place) for place in range(3))
        weights = weights_in[:, glob]
        delta = near_delta + jnp.sum(weights * prob_grad, axis=1, keepdims=True)
        score_grad = (weights * (prob_grad - delta)).astype(BF16)
        score_out[:, glob] = score_grad
        key_term = dot(score_grad, query[:, part], TN)
        keep_out[:, part] = jnp.where(odd, value_term[:, part], key_term)
        send_out[:slots, part] = jnp.where(odd, key_term, value_term[:, part]).astype(BF16)
        notes = (top, *thirds(scale), *thirds(delta))
        put_columns(stats, every, head, notes, step=heads, width=1)
        put_columns(delta_out, every, head, (delta,))

    lax.fori_loop(0, heads, one_head, None, unroll=2)
    groups, lines = note_lines(query.shape[0], query.shape[1])
    for start in range(0, query.shape[0], BLOCK):
        turned = stats[pl.ds(start, BLOCK), :].T
        for group in range(groups):
            at = pl.ds(group * query.shape[0] + start, BLOCK)
            send_out[slots:, at] = turned[group * lines : (group + 1) * lines].astype(BF16)


def rest_kernel(strides, cols_ref, weights_in, probs, deltas, glob_weights, scores_in, *refs):
    glob_key, glob_value, own_key, own_value = refs[:4]
    far_keys, far_values = refs[4 : 4 + strides], refs[4 + strides : 4 + 2 * strides]
    att_out, query_out = refs[-2:]
    blocks, heads = own_key.shape[0] // BLOCK, own_key.shape[1] // HEAD_SIZE
    near, slots = (strides + 1) * BLOCK, glob_key.shape[0]
    device = lax.axis_index("ctx")

    def one_head(head, _):
        part = columns_of(head)
        wide = pl.ds(pl.multiple_of(head * near, near), near)
        glob = pl.ds(pl.multiple_of(head * slots, slots), slots)
        for i in range(blocks):
            rows = pl.ds(i * BLOCK, BLOCK)
            keys = near_at(strides, device, blocks, i, cols_ref, own_key, far_keys, part)
            values = near_at(strides, device, blocks, i, cols_ref, own_value, far_values, part)
            delta = take_column(deltas, rows, head, 0)
            weights = weights_in[rows, wide]
            score_grad = (weights * (probs[rows, wide] - delta)).astype(BF16)
            attention = dot(weights.astype(BF16), values)
            attention = attention + dot(glob_weights[rows, glob].astype(BF16), glob_value[:, part])
            att_out[rows, part] = attention.astype(BF16)
            query_sum = dot(score_grad, keys) + dot(scores_in[rows, glob], glob_key[:, part])
            query_out[rows, part] = (query_sum * FACTOR).astype(BF16)

    lax.fori_loop(0, heads, one_head, None, unroll=2)


def key_kernel(s, count, cols_ref, key, value, *refs):
    *pair, message = refs[: count + 1]
    so_far, (key_out, value_out, stats) = refs[count + 1 : -3], refs[-3:]
    blocks = key.shape[0] // BLOCK
    heads = key.shape[1] // HEAD_SIZE
    device = lax.axis_index("ctx")
    read_notes(message, stats, key.shape[0], heads)
    grad_start = 0 if count > 1 else pair[0].shape[0] // 2

    def one_head(head, _):
        part = columns_of(head)
        stat_at = pl.multiple_of(head * STAT_ROWS, STAT_ROWS)
        if so_far:
            key_out[:, part] = so_far[0][:, part]
            value_out[:, part] = so_far[1][:, part]
        for i in range(blocks):
            rows = pl.ds(i * BLOCK, BLOCK)
            if s < 0:
                place = rows
            else:
                partner = jnp.bitwise_xor(device, 1 << s)
                place = block_at(cols_ref[s, partner * blocks + i] - device * blocks)
            q = pair[0][rows, part]
            g = pair[-1][pl.ds(grad_start + i * BLOCK, BLOCK), part]
            stat = stats[pl.ds(stat_at, STAT_ROWS), rows]
            top, scale, delta = stat[0:1], stat[1:2], stat[2:3]
            weights = jnp.exp(dot(key[place, part], q, NT) * FACTOR - top) * scale
            prob_grad = dot(value[place, part], g, NT)
            score_grad = (weights * (prob_grad - delta)).astype(BF16)
            key_term = dot(score_grad, q)
            value_term = dot(weights.astype(BF16), g)
            if s < 0:
                key_out[place, part] = key_term
                value_out[place, part] = value_term
            else:
                key_out[place, part] += key_term
                value_out[place, part] += value_term

    lax.fori_loop(0, heads, one_head, None)


def key_side(source, cols, key, value, pair, message, so_far=()):
    shape = like(key.shape, F32)
    heads = key.shape[1] // HEAD_SIZE
    return call(
        functools.partial(key_kernel, source, len(pair)),
        [shape, shape],
        cols,
        key,
        value,
        *pair,
        message,
        *so_far,
        scalars=1,
        scratch=[pltpu.VMEM((heads * STAT_ROWS, key.shape[0]), F32)],
    )


def bit_of(mask):
    return jnp.bitwise_and(lax.axis_index("ctx"), mask) != 0


def add_kernel(cut, last, total, got, mine, *outs):
    slots = total.shape[0]
    result = total[...] + got[:slots, :].astype(F32)
    send = result
    if cut:
        low, high, upper = result[: slots // 2], result[slots // 2 :], bit_of(cut)
        result, send = jnp.where(upper, high, low), jnp.where(upper, low, high)
    if last:
        outs[0][...] = result.astype(BF16)
    else:
        outs[0][...] = result
        outs[1][: send.shape[0], :] = send.astype(BF16)
        outs[1][send.shape[0] :, :] = mine[mine.shape[0] - outs[1].shape[0] + send.shape[0] :, :]


def add(total, got, mine, notes, cut=0, last=False):
    slots, width = total.shape
    slots = slots // 2 if cut else slots
    shapes = [like((slots, width))]
    if not last:
        shapes = [like((slots, width), F32), like((slots + notes, width))]
    return call(functools.partial(add_kernel, cut, last), shapes, total, got, mine)


def out_kernel(*refs):
    refs[-1][...] = sum((ref[...].astype(F32) for ref in refs[1:-1]), refs[0][...]).astype(BF16)


def final_kernel(cut, scatter, key, value, *refs):
    half = len(refs) // 2 - 1
    kept, got, (key_out, value_out) = refs[:half], refs[half:-2], refs[-2:]
    odd = bit_of(1)

    def rows_of(parts):
        if len(parts) == 1:
            return dot(scatter[...], parts[0][...])
        mine, other, upper = parts[0][...].astype(F32), parts[1][...].astype(F32), bit_of(cut)
        whole = [jnp.where(upper, other, mine), jnp.where(upper, mine, other)]
        return dot(scatter[...], jnp.concatenate(whole, 0).astype(BF16))

    kept_rows, got_rows = rows_of(kept), rows_of(got)
    key_rows = jnp.where(odd, got_rows, kept_rows)
    value_rows = jnp.where(odd, kept_rows, got_rows)
    key_out[...] = ((key[...] + key_rows) * FACTOR).astype(BF16)
    value_out[...] = (value[...] + value_rows).astype(BF16)


def finish(cut, scatter, key, value, kept, got):
    shape = jax.ShapeDtypeStruct(key.shape, BF16)
    kernel = functools.partial(final_kernel, cut)
    return call(kernel, [shape, shape], scatter, key, value, *kept, *got)


def per_device(query_act, key_act, value_act, out_weight, cotangent, butterfly_cols, global_cols):
    strides = butterfly_cols.shape[1]
    groups = lax.axis_size("head")
    cube = strides == 3 and lax.axis_size("ctx") == 1 << strides
    cols = butterfly_cols.T
    slots = global_cols.shape[0]
    rows, width = key_act.shape
    masks = [1 << s for s in range(strides)]
    held = (0, *masks) if cube else (0,)
    owners = ((3, 5), (6, 7)) if cube else ()

    scatter, *hot = call(
        functools.partial(hot_kernel, held, owners),
        [like((rows, slots))]
        + [like((slots, rows))] * len(held)
        + [like((slots, HEAD_SIZE), F32)] * len(owners),
        global_cols.reshape(1, -1),
    )
    selects, owned = hot[: len(held)], hot[len(held) :]
    near_keys = [key_act] + [swap(key_act, "ctx", m) for m in masks]
    near_values = [value_act] + [swap(value_act, "ctx", m) for m in masks]
    pieces = [cotangent] + [swap(cotangent, "head", m) for m in range(1, groups)]
    if cube:
        glob = []
        for near in (near_keys, near_values):
            have = select_globals(selects, near)
            have = merge(have, swap(have, "ctx", 1), owned[0])
            glob.append([have, swap(have, "ctx", 2)])
        glob_keys, glob_values = glob
    else:
        parts = (select_globals(selects, [key_act]), select_globals(selects, [value_act]))
        glob_keys, glob_values = ([part] for part in lax.psum(parts, "ctx"))
    attn_grad, pair = call(
        grad_kernel, [like((rows, width)), like((2 * rows, width))], out_weight, query_act, *pieces
    )
    pairs = [[pair]] + [[swap(pair, "ctx", m)] for m in masks[:-1]]
    m = masks[-1]
    pairs.append([swap(query_act, "ctx", m), swap(attn_grad, "ctx", m)])
    near_all = [key_act, value_act, *near_keys[1:], *near_values[1:]]
    heads = width // HEAD_SIZE
    near = (strides + 1) * BLOCK
    weights, probs, glob_weights, value_term, glob_key, near_stats = call(
        functools.partial(near_kernel, strides, len(glob_keys)),
        [
            like((rows, heads * near), F32),
            like((rows, heads * near), F32),
            like((rows, heads * slots), F32),
            like((slots, width), F32),
            like((slots, width)),
            like((rows, BLOCK), F32),
        ],
        cols,
        query_act,
        attn_grad,
        *near_all,
        *glob_keys,
        *owned[1:],
        scalars=1,
    )
    total, message, deltas, scores, glob_value = call(
        functools.partial(glob_kernel, len(glob_values)),
        [
            like((slots, width), F32),
            like((slots + note_lines(rows, width)[1], width)),
            like((rows, BLOCK), F32),
            like((rows, heads * slots)),
            like((slots, width)),
        ],
        query_act,
        attn_grad,
        near_stats,
        glob_weights,
        value_term,
        *glob_values,
        *owned[1:],
        scratch=[pltpu.VMEM((rows, BLOCK), F32)],
    )
    attention, query_grad = call(
        functools.partial(rest_kernel, strides),
        [like((rows, width)), jax.ShapeDtypeStruct((rows, width), BF16)],
        cols,
        weights,
        probs,
        deltas,
        glob_weights,
        scores,
        glob_key,
        glob_value,
        *near_all,
        scalars=1,
    )
    messages = [message]
    if cube:
        notes = note_lines(rows, width)[1]
        messages.append(swap(message, "ctx", 1))
        total, message = add(total, messages[1], messages[0], notes, cut=2)
        messages.append(swap(message, "ctx", 2))
        total, message = add(total, messages[2], messages[0], notes)
        messages.append(swap(message, "ctx", 4))
        (mine,) = add(total, messages[3], messages[0], notes, last=True)
        other = swap(mine, "ctx", 2)
        kept = [mine, other]
        got = [swap(mine, "ctx", 1), swap(other, "ctx", 1)]
    else:
        messages += [swap(message, "ctx", m) for m in masks]
        odd = jnp.bitwise_and(lax.axis_index("ctx"), 1) == 1
        send = message[:slots].astype(F32)
        key_term, value_term = lax.psum(
            (jnp.where(odd, send, total), jnp.where(odd, total, send)), "ctx"
        )
        kept = [jnp.where(odd, value_term, key_term).astype(BF16)]
        got = [jnp.where(odd, key_term, value_term).astype(BF16)]
    term = out_weight.shape[1] // groups
    shapes = [like((rows, term), F32 if m == 0 else BF16) for m in range(groups)]
    terms = call(project_kernel, shapes, attention, out_weight)
    parts = [swap(terms[m], "head", m) for m in range(1, groups)]
    out_shape = jax.ShapeDtypeStruct((rows, term), BF16)
    layer_out = call(out_kernel, [out_shape], terms[0], *parts)[0]
    so_far = ()
    for at, m in enumerate([0, *masks]):
        so_far = key_side(at - 1, cols, key_act, value_act, pairs[at], messages[at], so_far)
    key_sum, value_sum = so_far
    key_grad, value_grad = finish(2, scatter, key_sum, value_sum, kept, got)
    return (layer_out, query_grad, key_grad, value_grad)


def solution(mesh):
    in_specs = (
        P("ctx", "head"),
        P("ctx", "head"),
        P("ctx", "head"),
        P("head", None),
        P("ctx", "head"),
        P(),
        P(),
    )
    out_specs = (P("ctx", "head"),) * 4

    return jax.shard_map(
        per_device, mesh=mesh, in_specs=in_specs, out_specs=out_specs, check_vma=False
    )
```

profile of v0, /device:TPU:0, one launch (start us, length us, event | category | flops | bytes accessed | tf_op | source)
XLA Modules:
  0.0 113.6 jit_solution(3063554303170426007)
XLA Ops:
  0.6 3.1 %collective-permute-start.3 = (bf16[256,512]{1,0:T(8,128)(2,1)}, bf16[256,512]{1,0:T(8,128)(2,1)S(1)}, u32[]{:S(2)}, u32[]{:S(2)}) collective-permute-start(bf16[256,512]{1,0:T(8,128)(2,1)} %key.7), channel_id=1, source_target_pairs={{0,4},{4,0},{8,12},{12,8},{16,20},{20,16},{24,28},{28,24},{1,5},{5... | collective-permute-start | bytes 786440 | tf_op jit(solution)/shard_map/ppermute | solution.py:26
  3.7 1.6 %collective-permute-start.4 = (bf16[256,512]{1,0:T(8,128)(2,1)}, bf16[256,512]{1,0:T(8,128)(2,1)S(1)}, u32[]{:S(2)}, u32[]{:S(2)}) collective-permute-start(bf16[256,512]{1,0:T(8,128)(2,1)} %key.7), channel_id=1, source_target_pairs={{0,8},{4,12},{8,0},{12,4},{16,24},{20,28},{24,16},{28,20},{1,9},{5... | collective-permute-start | bytes 786440 | tf_op jit(solution)/shard_map/ppermute | solution.py:26
  5.3 2.6 %collective-permute-start.5 = (bf16[256,512]{1,0:T(8,128)(2,1)}, bf16[256,512]{1,0:T(8,128)(2,1)S(1)}, u32[]{:S(2)}, u32[]{:S(2)}) collective-permute-start(bf16[256,512]{1,0:T(8,128)(2,1)} %key.7), channel_id=1, source_target_pairs={{0,16},{4,20},{8,24},{12,28},{16,0},{20,4},{24,8},{28,12},{1,17},{... | collective-permute-start | bytes 786440 | tf_op jit(solution)/shard_map/ppermute | solution.py:26
  7.9 0.5 collective-permute-start.6
  8.4 0.4 collective-permute-start.7
  8.8 1.9 %collective-permute-done.3.refs_5_.refs_2_.refs_4_ = bf16[256,512]{1,0:T(8,128)(2,1)S(1)} collective-permute-done((bf16[256,512]{1,0:T(8,128)(2,1)}, bf16[256,512]{1,0:T(8,128)(2,1)S(1)}, u32[]{:S(2)}, u32[]{:S(2)}) %collective-permute-start.3) | collective-permute-done | bytes 262176 | tf_op jit(solution)/shard_map/ppermute | solution.py:26
  10.8 3.4 %collective-permute-start.8 = (bf16[256,512]{1,0:T(8,128)(2,1)}, bf16[256,512]{1,0:T(8,128)(2,1)S(1)}, u32[]{:S(2)}, u32[]{:S(2)}) collective-permute-start(bf16[256,512]{1,0:T(8,128)(2,1)} %value.7), channel_id=1, source_target_pairs={{0,16},{4,20},{8,24},{12,28},{16,0},{20,4},{24,8},{28,12},{1,17},{... | collective-permute-start | bytes 786440 | tf_op jit(solution)/shard_map/ppermute | solution.py:26
  14.1 0.7 copy-done.8
  15.1 4.0 %collective-permute-done.4.refs_6_.refs_3_.refs_5_ = bf16[256,512]{1,0:T(8,128)(2,1)S(1)} collective-permute-done((bf16[256,512]{1,0:T(8,128)(2,1)}, bf16[256,512]{1,0:T(8,128)(2,1)S(1)}, u32[]{:S(2)}, u32[]{:S(2)}) %collective-permute-start.4) | collective-permute-done | bytes 262176 | tf_op jit(solution)/shard_map/ppermute | solution.py:26
  19.1 1.6 %collective-permute-done.5.refs_7_.refs_4_.refs_6_ = bf16[256,512]{1,0:T(8,128)(2,1)S(1)} collective-permute-done((bf16[256,512]{1,0:T(8,128)(2,1)}, bf16[256,512]{1,0:T(8,128)(2,1)S(1)}, u32[]{:S(2)}, u32[]{:S(2)}) %collective-permute-start.5) | collective-permute-done | bytes 262176 | tf_op jit(solution)/shard_map/ppermute | solution.py:26
  20.7 0.9 copy-done
  21.7 0.4 shard_map.104.have
  22.2 6.2 %collective-permute-done.7.refs_6_.refs_8_ = bf16[256,512]{1,0:T(8,128)(2,1)S(1)} collective-permute-done((bf16[256,512]{1,0:T(8,128)(2,1)}, bf16[256,512]{1,0:T(8,128)(2,1)S(1)}, u32[]{:S(2)}, u32[]{:S(2)}) %collective-permute-start.7) | collective-permute-done | bytes 262176 | tf_op jit(solution)/shard_map/ppermute | solution.py:26
  28.4 2.4 %collective-permute-done.8.refs_7_.refs_9_ = bf16[256,512]{1,0:T(8,128)(2,1)S(1)} collective-permute-done((bf16[256,512]{1,0:T(8,128)(2,1)}, bf16[256,512]{1,0:T(8,128)(2,1)S(1)}, u32[]{:S(2)}, u32[]{:S(2)}) %collective-permute-start.8) | collective-permute-done | bytes 262176 | tf_op jit(solution)/shard_map/ppermute | solution.py:26
  30.8 0.9 copy-done.2
  31.8 0.4 shard_map.107.have
  32.2 0.6 collective-permute-start.11
  32.8 1.5 %collective-permute-start.1 = (bf16[256,512]{1,0:T(8,128)(2,1)S(1)}, bf16[256,512]{1,0:T(8,128)(2,1)S(1)}, u32[]{:S(2)}, u32[]{:S(2)}) collective-permute-start(bf16[256,512]{1,0:T(8,128)(2,1)S(1)} %copy-done.6), channel_id=1, source_target_pairs={{0,2},{1,3},{2,0},{3,1},{4,6},{5,7},{6,4},{7,5},{8,10},{9,11},{10,... | collective-permute-start | bytes 786440 | tf_op jit(solution)/shard_map/ppermute | solution.py:26
  34.3 0.4 collective-permute-start.2
  34.8 0.5 collective-permute-start.10
  35.3 3.4 %collective-permute-done.11.got = bf16[256,512]{1,0:T(8,128)(2,1)S(1)} collective-permute-done((bf16[256,512]{1,0:T(8,128)(2,1)S(1)}, bf16[256,512]{1,0:T(8,128)(2,1)S(1)}, u32[]{:S(2)}, u32[]{:S(2)}) %collective-permute-start.11) | collective-permute-done | bytes 262176 | tf_op jit(solution)/shard_map/ppermute | solution.py:26
  38.8 1.0 collective-permute-start.12
  39.7 2.2 %collective-permute-done.1.refs_2_ = bf16[256,512]{1,0:T(8,128)(2,1)S(1)} collective-permute-done((bf16[256,512]{1,0:T(8,128)(2,1)S(1)}, bf16[256,512]{1,0:T(8,128)(2,1)S(1)}, u32[]{:S(2)}, u32[]{:S(2)}) %collective-permute-start.1) | collective-permute-done | bytes 262176 | tf_op jit(solution)/shard_map/ppermute | solution.py:26
  42.0 4.7 %collective-permute-done.2.refs_3_ = bf16[256,512]{1,0:T(8,128)(2,1)S(1)} collective-permute-done((bf16[256,512]{1,0:T(8,128)(2,1)S(1)}, bf16[256,512]{1,0:T(8,128)(2,1)S(1)}, u32[]{:S(2)}, u32[]{:S(2)}) %collective-permute-start.2) | collective-permute-done | bytes 262176 | tf_op jit(solution)/shard_map/ppermute | solution.py:26
  46.7 0.7 shard_map.102
  47.4 1.6 %collective-permute-start.22 = (bf16[512,512]{1,0:T(8,128)(2,1)S(1)}, bf16[512,512]{1,0:T(8,128)(2,1)S(1)}, u32[]{:S(2)}, u32[]{:S(2)}) collective-permute-start(bf16[512,512]{1,0:T(8,128)(2,1)S(1)} %get-tuple-element.72.refs_0_), channel_id=1, source_target_pairs={{0,4},{4,0},{8,12},{12,8},{16,20},{20,16},{24,28},{28,24},{1,5},{5... | collective-permute-start | bytes 1572872 | tf_op jit(solution)/shard_map/ppermute | solution.py:26
  49.0 3.5 %shard_map.106 = (f32[256,2048]{1,0:T(8,128)S(1)}, f32[256,2048]{1,0:T(8,128)S(1)}, f32[256,1024]{1,0:T(8,128)S(1)}, f32[256,512]{1,0:T(8,128)S(1)}, bf16[256,51...) custom-call(s32[3,16]{1,0:T(4,128)S(1)} %bitcast.2, bf16[256,512]{1,0:T(8,128)(2,1)S(1)} %copy-done.5, ...), custom_call_target="tpu_custom_call" | custom-call | tf_op jit(solution)/shard_map/pallas_call | solution.py:34
  52.5 2.1 %shard_map.109 = (f32[256,512]{1,0:T(8,128)S(1)}, bf16[272,512]{1,0:T(8,128)(2,1)S(1)}, f32[256,128]{1,0:T(8,128)S(1)}, bf16[256,1024]{1,0:T(8,128)(2,1)S(1)}, bf16[256,512]{1,0:T(8,128)(2,1)S(1)}) custom-call(bf16[256,512]{1,0:T(8,128)(2,1)S(1)} %copy-done.5, bf16[256,512]{1,0:T(8,128)(2,1)S(1)} %get-tuple-element.44.grad, ...), custom_call_target="tpu_custom_call" | custom-call | tf_op jit(solution)/shard_map/pallas_call | solution.py:34
  54.6 0.6 collective-permute-start.18
  55.1 12.7 %collective-permute-done.18.got.refs_1_ = bf16[272,512]{1,0:T(8,128)(2,1)S(1)} collective-permute-done((bf16[272,512]{1,0:T(8,128)(2,1)S(1)}, bf16[272,512]{1,0:T(8,128)(2,1)S(1)}, u32[]{:S(2)}, u32[]{:S(2)}) %collective-permute-start.18) | collective-permute-done | bytes 278560 | tf_op jit(solution)/shard_map/ppermute | solution.py:26
  67.9 0.5 collective-permute-start.19
  68.4 1.6 %collective-permute-start.21 = (bf16[512,512]{1,0:T(8,128)(2,1)S(1)}, bf16[512,512]{1,0:T(8,128)(2,1)S(1)}, u32[]{:S(2)}, u32[]{:S(2)}) collective-permute-start(bf16[512,512]{1,0:T(8,128)(2,1)S(1)} %get-tuple-element.72.refs_0_), channel_id=1, source_target_pairs={{0,8},{4,12},{8,0},{12,4},{16,24},{20,28},{24,16},{28,20},{1,9},{5... | collective-permute-start | bytes 1572872 | tf_op jit(solution)/shard_map/ppermute | solution.py:26
  70.0 2.6 %shard_map.110 = (bf16[256,512]{1,0:T(8,128)(2,1)S(1)}, bf16[256,512]{1,0:T(8,128)(2,1)}) custom-call(s32[3,16]{1,0:T(4,128)S(1)} %bitcast.3, f32[256,2048]{1,0:T(8,128)S(1)} %get-tuple-element.51.weights_in, f32[256,2048]{1,0:T(8,128)S(1)} %get-tuple-element.52.probs, f32[256,128]{1,0:T(8,128)S(1)} %get-tuple-element.56.deltas, ...), custom_call_target="tpu_custom_call" | custom-call | tf_op jit(solution)/shard_map/pallas_call | solution.py:34
  72.6 0.7 shard_map.111
  73.4 1.6 %collective-permute-start.14 = (bf16[256,512]{1,0:T(8,128)(2,1)S(1)}, bf16[256,512]{1,0:T(8,128)(2,1)S(1)}, u32[]{:S(2)}, u32[]{:S(2)}) collective-permute-start(bf16[256,512]{1,0:T(8,128)(2,1)S(1)} %get-tuple-element.63), channel_id=1, source_target_pairs={{0,2},{1,3},{2,0},{3,1},{4,6},{5,7},{6,4},{7,5},{8,10},{9,11},{10,... | collective-permute-start | bytes 786440 | tf_op jit(solution)/shard_map/ppermute | solution.py:26
  75.0 1.1 %collective-permute-start.20 = (bf16[144,512]{1,0:T(8,128)(2,1)S(1)}, bf16[144,512]{1,0:T(8,128)(2,1)S(1)}, u32[]{:S(2)}, u32[]{:S(2)}) collective-permute-start(bf16[144,512]{1,0:T(8,128)(2,1)S(1)} %get-tuple-element.71), channel_id=1, source_target_pairs={{0,16},{4,20},{8,24},{12,28},{16,0},{20,4},{24,8},{28,12},{1,17},{... | collective-permute-start | bytes 442376 | tf_op jit(solution)/shard_map/ppermute | solution.py:26
  76.2 1.9 %collective-permute-start.16 = (bf16[256,512]{1,0:T(8,128)(2,1)S(1)}, bf16[256,512]{1,0:T(8,128)(2,1)S(1)}, u32[]{:S(2)}, u32[]{:S(2)}) collective-permute-start(bf16[256,512]{1,0:T(8,128)(2,1)S(1)} %copy-done.5), channel_id=1, source_target_pairs={{0,16},{4,20},{8,24},{12,28},{16,0},{20,4},{24,8},{28,12},{1,17},{... | collective-permute-start | bytes 786440 | tf_op jit(solution)/shard_map/ppermute | solution.py:26
  78.1 9.0 %collective-permute-done.20.refs_2_.got = bf16[144,512]{1,0:T(8,128)(2,1)S(1)} collective-permute-done((bf16[144,512]{1,0:T(8,128)(2,1)S(1)}, bf16[144,512]{1,0:T(8,128)(2,1)S(1)}, u32[]{:S(2)}, u32[]{:S(2)}) %collective-permute-start.20) | collective-permute-done | bytes 147488 | tf_op jit(solution)/shard_map/ppermute | solution.py:26
  87.1 3.4 %collective-permute-start.17 = (bf16[256,512]{1,0:T(8,128)(2,1)S(1)}, bf16[256,512]{1,0:T(8,128)(2,1)S(1)}, u32[]{:S(2)}, u32[]{:S(2)}) collective-permute-start(bf16[256,512]{1,0:T(8,128)(2,1)S(1)} %get-tuple-element.44.grad), channel_id=1, source_target_pairs={{0,16},{4,20},{8,24},{12,28},{16,0},{20,4},{24,8},{28,12},{1,17},{... | collective-permute-start | bytes 786440 | tf_op jit(solution)/shard_map/ppermute | solution.py:26
  90.7 1.6 %collective-permute-start.24 = (bf16[128,512]{1,0:T(8,128)(2,1)S(1)}, bf16[128,512]{1,0:T(8,128)(2,1)S(1)}, u32[]{:S(2)}, u32[]{:S(2)}) collective-permute-start(bf16[128,512]{1,0:T(8,128)(2,1)S(1)} %shard_map.119.refs_0_), channel_id=1, source_target_pairs={{0,4},{4,0},{8,12},{12,8},{16,20},{20,16},{24,28},{28,24},{1,5},{5... | collective-permute-start | bytes 393224 | tf_op jit(solution)/shard_map/ppermute | solution.py:26
  92.3 7.7 %collective-permute-done.23.refs_1_ = bf16[128,512]{1,0:T(8,128)(2,1)S(1)} collective-permute-done((bf16[128,512]{1,0:T(8,128)(2,1)S(1)}, bf16[128,512]{1,0:T(8,128)(2,1)S(1)}, u32[]{:S(2)}, u32[]{:S(2)}) %collective-permute-start.23) | collective-permute-done | bytes 131104 | tf_op jit(solution)/shard_map/ppermute | solution.py:26
  99.9 1.5 %collective-permute-start.25 = (bf16[128,512]{1,0:T(8,128)(2,1)S(1)}, bf16[128,512]{1,0:T(8,128)(2,1)S(1)}, u32[]{:S(2)}, u32[]{:S(2)}) collective-permute-start(bf16[128,512]{1,0:T(8,128)(2,1)S(1)} %collective-permute-done.23.refs_1_), channel_id=1, source_target_pairs={{0,4},{4,0},{8,12},{12,8},{16,20},{20,16},{24,28},{28,24},{1,5},{5... | collective-permute-start | bytes 393224 | tf_op jit(solution)/shard_map/ppermute | solution.py:26
  101.4 2.5 %shard_map.115 = (f32[256,512]{1,0:T(8,128)S(1)}, f32[256,512]{1,0:T(8,128)S(1)}) custom-call(s32[3,16]{1,0:T(4,128)S(1)} %bitcast.4, bf16[256,512]{1,0:T(8,128)(2,1)S(1)} %copy-done.1, bf16[256,512]{1,0:T(8,128)(2,1)S(1)} %copy-done.3, bf16[512,512]{1,0:T(8,128)(2,1)S(1)} %get-tuple-element.72.refs_0_, bf16[272,512]{1,0:T(8,128)(2,1)S(1)} %get-tuple-element.68.mine.refs_1_), custom_call_target="tpu_custom_call" | custom-call | tf_op jit(solution)/shard_map/pallas_call | solution.py:34
  103.9 0.8 shard_map.112
  104.8 2.5 %shard_map.116 = (f32[256,512]{1,0:T(8,128)S(1)}, f32[256,512]{1,0:T(8,128)S(1)}) custom-call(s32[3,16]{1,0:T(4,128)S(1)} %bitcast.5, bf16[256,512]{1,0:T(8,128)(2,1)S(1)} %copy-done.1, bf16[256,512]{1,0:T(8,128)(2,1)S(1)} %copy-done.3, bf16[512,512]{1,0:T(8,128)(2,1)S(1)} %collective-permute-done.22.refs_0_, ...), custom_call_target="tpu_custom_call" | custom-call | tf_op jit(solution)/shard_map/pallas_call | solution.py:34
  107.3 2.5 %shard_map.117 = (f32[256,512]{1,0:T(8,128)S(1)}, f32[256,512]{1,0:T(8,128)S(1)}) custom-call(s32[3,16]{1,0:T(4,128)S(1)} %bitcast.6, bf16[256,512]{1,0:T(8,128)(2,1)S(1)} %copy-done.1, bf16[256,512]{1,0:T(8,128)(2,1)S(1)} %copy-done.3, bf16[512,512]{1,0:T(8,128)(2,1)S(1)} %collective-permute-done.21.refs_0_, ...), custom_call_target="tpu_custom_call" | custom-call | tf_op jit(solution)/shard_map/pallas_call | solution.py:34
  109.8 2.5 %shard_map.118 = (f32[256,512]{1,0:T(8,128)S(1)}, f32[256,512]{1,0:T(8,128)S(1)}) custom-call(s32[3,16]{1,0:T(4,128)S(1)} %bitcast.7, bf16[256,512]{1,0:T(8,128)(2,1)S(1)} %copy-done.1, bf16[256,512]{1,0:T(8,128)(2,1)S(1)} %copy-done.3, bf16[256,512]{1,0:T(8,128)(2,1)S(1)} %collective-permute-done.16.refs_0_, ...), custom_call_target="tpu_custom_call" | custom-call | tf_op jit(solution)/shard_map/pallas_call | solution.py:34
  112.4 1.2 %shard_map.120 = (bf16[256,512]{1,0:T(8,128)(2,1)}, bf16[256,512]{1,0:T(8,128)(2,1)}) custom-call(bf16[256,256]{1,0:T(8,128)(2,1)S(1)} %get-tuple-element.66.scatter, f32[256,512]{1,0:T(8,128)S(1)} %get-tuple-element.79.key, f32[256,512]{1,0:T(8,128)S(1)} %get-tuple-element.80.value, bf16[128,512]{1,0:T(8,128)(2,1)S(1)} %shard_map.119.refs_0_, ...), custom_call_target="tpu_custom_call" | custom-call | tf_op jit(solution)/shard_map/pallas_call | solution.py:34
  (41 shorter events, 0.9 us)
Async XLA Ops:
  0.6 10.1 %collective-permute-start.3 = (bf16[256,512]{1,0:T(8,128)(2,1)}, bf16[256,512]{1,0:T(8,128)(2,1)S(1)}, u32[]{:S(2)}, u32[]{:S(2)}) collective-permute-start(bf16[256,512]{1,0:T(8,128)(2,1)} %key.7), channel_id=1, source_target_pairs={{0,4},{4,0},{8,12},{12,8},{16,20},{20,16},{24,28},{28,24},{1,5},{5... | collective-permute-start | bytes 786440 | tf_op jit(solution)/shard_map/ppermute | solution.py:26
  3.7 15.4 %collective-permute-start.4 = (bf16[256,512]{1,0:T(8,128)(2,1)}, bf16[256,512]{1,0:T(8,128)(2,1)S(1)}, u32[]{:S(2)}, u32[]{:S(2)}) collective-permute-start(bf16[256,512]{1,0:T(8,128)(2,1)} %key.7), channel_id=1, source_target_pairs={{0,8},{4,12},{8,0},{12,4},{16,24},{20,28},{24,16},{28,20},{1,9},{5... | collective-permute-start | bytes 786440 | tf_op jit(solution)/shard_map/ppermute | solution.py:26
  5.3 15.4 %collective-permute-start.5 = (bf16[256,512]{1,0:T(8,128)(2,1)}, bf16[256,512]{1,0:T(8,128)(2,1)S(1)}, u32[]{:S(2)}, u32[]{:S(2)}) collective-permute-start(bf16[256,512]{1,0:T(8,128)(2,1)} %key.7), channel_id=1, source_target_pairs={{0,16},{4,20},{8,24},{12,28},{16,0},{20,4},{24,8},{28,12},{1,17},{... | collective-permute-start | bytes 786440 | tf_op jit(solution)/shard_map/ppermute | solution.py:26
  7.9 14.3 %collective-permute-start.6 = (bf16[256,512]{1,0:T(8,128)(2,1)}, bf16[256,512]{1,0:T(8,128)(2,1)S(1)}, u32[]{:S(2)}, u32[]{:S(2)}) collective-permute-start(bf16[256,512]{1,0:T(8,128)(2,1)} %value.7), channel_id=1, source_target_pairs={{0,4},{4,0},{8,12},{12,8},{16,20},{20,16},{24,28},{28,24},{1,5},{5... | collective-permute-start | bytes 786440 | tf_op jit(solution)/shard_map/ppermute | solution.py:26
  8.4 20.0 %collective-permute-start.7 = (bf16[256,512]{1,0:T(8,128)(2,1)}, bf16[256,512]{1,0:T(8,128)(2,1)S(1)}, u32[]{:S(2)}, u32[]{:S(2)}) collective-permute-start(bf16[256,512]{1,0:T(8,128)(2,1)} %value.7), channel_id=1, source_target_pairs={{0,8},{4,12},{8,0},{12,4},{16,24},{20,28},{24,16},{28,20},{1,9},{5... | collective-permute-start | bytes 786440 | tf_op jit(solution)/shard_map/ppermute | solution.py:26
  10.8 20.1 %collective-permute-start.8 = (bf16[256,512]{1,0:T(8,128)(2,1)}, bf16[256,512]{1,0:T(8,128)(2,1)S(1)}, u32[]{:S(2)}, u32[]{:S(2)}) collective-permute-start(bf16[256,512]{1,0:T(8,128)(2,1)} %value.7), channel_id=1, source_target_pairs={{0,16},{4,20},{8,24},{12,28},{16,0},{20,4},{24,8},{28,12},{1,17},{... | collective-permute-start | bytes 786440 | tf_op jit(solution)/shard_map/ppermute | solution.py:26
  14.1 0.7 copy-start.8
  20.7 1.0 copy-start
  21.7 11.1 %copy-start.6 = (bf16[256,512]{1,0:T(8,128)(2,1)S(1)}, bf16[256,512]{1,0:T(8,128)(2,1)}, u32[]{:S(2)}) copy-start(bf16[256,512]{1,0:T(8,128)(2,1)} %refs_0_.2) | copy-start | bytes 786436
  21.7 25.0 %copy-start.5 = (bf16[256,512]{1,0:T(8,128)(2,1)S(1)}, bf16[256,512]{1,0:T(8,128)(2,1)}, u32[]{:S(2)}) copy-start(bf16[256,512]{1,0:T(8,128)(2,1)} %query.5) | copy-start | bytes 786436
  22.1 12.5 %collective-permute-start.9 = (bf16[256,512]{1,0:T(8,128)(2,1)S(1)}, bf16[256,512]{1,0:T(8,128)(2,1)S(1)}, u32[]{:S(2)}, u32[]{:S(2)}) collective-permute-start(bf16[256,512]{1,0:T(8,128)(2,1)S(1)} %shard_map.104.have), channel_id=1, source_target_pairs={{0,4},{4,0},{8,12},{12,8},{16,20},{20,16},{24,28},{28,24},{1,5},{5... | collective-permute-start | bytes 786440 | tf_op jit(solution)/shard_map/ppermute | solution.py:26
  30.8 1.0 copy-start.2
  31.8 14.9 %copy-start.4 = (bf16[512,2048]{1,0:T(8,128)(2,1)S(1)}, bf16[512,2048]{1,0:T(8,128)(2,1)}, u32[]{:S(2)}) copy-start(bf16[512,2048]{1,0:T(8,128)(2,1)} %weight_ref.3) | copy-start | bytes 6291460
  32.2 6.4 %collective-permute-start.11 = (bf16[256,512]{1,0:T(8,128)(2,1)S(1)}, bf16[256,512]{1,0:T(8,128)(2,1)S(1)}, u32[]{:S(2)}, u32[]{:S(2)}) collective-permute-start(bf16[256,512]{1,0:T(8,128)(2,1)S(1)} %shard_map.107.have), channel_id=1, source_target_pairs={{0,4},{4,0},{8,12},{12,8},{16,20},{20,16},{24,28},{28,24},{1,5},{5... | collective-permute-start | bytes 786440 | tf_op jit(solution)/shard_map/ppermute | solution.py:26
  32.8 6.9 %collective-permute-start = (bf16[256,512]{1,0:T(8,128)(2,1)S(1)}, bf16[256,512]{1,0:T(8,128)(2,1)S(1)}, u32[]{:S(2)}, u32[]{:S(2)}) collective-permute-start(bf16[256,512]{1,0:T(8,128)(2,1)S(1)} %copy-done.6), channel_id=1, source_target_pairs={{0,1},{1,0},{2,3},{3,2},{4,5},{5,4},{6,7},{7,6},{8,9},{9,8},{10,11... | collective-permute-start | bytes 786440 | tf_op jit(solution)/shard_map/ppermute | solution.py:26
  32.8 9.2 %collective-permute-start.1 = (bf16[256,512]{1,0:T(8,128)(2,1)S(1)}, bf16[256,512]{1,0:T(8,128)(2,1)S(1)}, u32[]{:S(2)}, u32[]{:S(2)}) collective-permute-start(bf16[256,512]{1,0:T(8,128)(2,1)S(1)} %copy-done.6), channel_id=1, source_target_pairs={{0,2},{1,3},{2,0},{3,1},{4,6},{5,7},{6,4},{7,5},{8,10},{9,11},{10,... | collective-permute-start | bytes 786440 | tf_op jit(solution)/shard_map/ppermute | solution.py:26
  34.3 12.4 %collective-permute-start.2 = (bf16[256,512]{1,0:T(8,128)(2,1)S(1)}, bf16[256,512]{1,0:T(8,128)(2,1)S(1)}, u32[]{:S(2)}, u32[]{:S(2)}) collective-permute-start(bf16[256,512]{1,0:T(8,128)(2,1)S(1)} %copy-done.6), channel_id=1, source_target_pairs={{0,3},{1,2},{2,1},{3,0},{4,7},{5,6},{6,5},{7,4},{8,11},{9,10},{10,... | collective-permute-start | bytes 786440 | tf_op jit(solution)/shard_map/ppermute | solution.py:26
  34.8 14.3 %copy-start.1 = (bf16[256,512]{1,0:T(8,128)(2,1)S(1)}, bf16[256,512]{1,0:T(8,128)(2,1)}, u32[]{:S(2)}) copy-start(bf16[256,512]{1,0:T(8,128)(2,1)} %key.7) | copy-start | bytes 786436
  34.8 14.2 %copy-start.3 = (bf16[256,512]{1,0:T(8,128)(2,1)S(1)}, bf16[256,512]{1,0:T(8,128)(2,1)}, u32[]{:S(2)}) copy-start(bf16[256,512]{1,0:T(8,128)(2,1)} %value.7) | copy-start | bytes 786436
  34.8 14.2 %copy-start.7 = (s32[16,3]{0,1:T(4,128)S(1)}, s32[16,3]{0,1:T(4,128)}, u32[]{:S(2)}) copy-start(s32[16,3]{0,1:T(4,128)} %param.12) | copy-start | bytes 580
  34.8 14.2 %collective-permute-start.10 = (bf16[256,512]{1,0:T(8,128)(2,1)S(1)}, bf16[256,512]{1,0:T(8,128)(2,1)S(1)}, u32[]{:S(2)}, u32[]{:S(2)}) collective-permute-start(bf16[256,512]{1,0:T(8,128)(2,1)S(1)} %shard_map.105.refs_8_), channel_id=1, source_target_pairs={{0,8},{4,12},{8,0},{12,4},{16,24},{20,28},{24,16},{28,20},{1,9},{5... | collective-permute-start | bytes 786440 | tf_op jit(solution)/shard_map/ppermute | solution.py:26
  38.8 13.8 %collective-permute-start.12 = (bf16[256,512]{1,0:T(8,128)(2,1)S(1)}, bf16[256,512]{1,0:T(8,128)(2,1)S(1)}, u32[]{:S(2)}, u32[]{:S(2)}) collective-permute-start(bf16[256,512]{1,0:T(8,128)(2,1)S(1)} %shard_map.108.refs_0_), channel_id=1, source_target_pairs={{0,8},{4,12},{8,0},{12,4},{16,24},{20,28},{24,16},{28,20},{1,9},{5... | collective-permute-start | bytes 786440 | tf_op jit(solution)/shard_map/ppermute | solution.py:26
  47.4 28.8 %collective-permute-start.22 = (bf16[512,512]{1,0:T(8,128)(2,1)S(1)}, bf16[512,512]{1,0:T(8,128)(2,1)S(1)}, u32[]{:S(2)}, u32[]{:S(2)}) collective-permute-start(bf16[512,512]{1,0:T(8,128)(2,1)S(1)} %get-tuple-element.72.refs_0_), channel_id=1, source_target_pairs={{0,4},{4,0},{8,12},{12,8},{16,20},{20,16},{24,28},{28,24},{1,5},{5... | collective-permute-start | bytes 1572872 | tf_op jit(solution)/shard_map/ppermute | solution.py:26
  54.6 13.3 %collective-permute-start.18 = (bf16[272,512]{1,0:T(8,128)(2,1)S(1)}, bf16[272,512]{1,0:T(8,128)(2,1)S(1)}, u32[]{:S(2)}, u32[]{:S(2)}) collective-permute-start(bf16[272,512]{1,0:T(8,128)(2,1)S(1)} %get-tuple-element.68.mine.refs_1_), channel_id=1, source_target_pairs={{0,4},{4,0},{8,12},{12,8},{16,20},{20,16},{24,28},{28,24},{1,5},{5... | collective-permute-start | bytes 835592 | tf_op jit(solution)/shard_map/ppermute | solution.py:26
  67.9 7.1 %collective-permute-start.19 = (bf16[144,512]{1,0:T(8,128)(2,1)S(1)}, bf16[144,512]{1,0:T(8,128)(2,1)S(1)}, u32[]{:S(2)}, u32[]{:S(2)}) collective-permute-start(bf16[144,512]{1,0:T(8,128)(2,1)S(1)} %get-tuple-element.70), channel_id=1, source_target_pairs={{0,8},{4,12},{8,0},{12,4},{16,24},{20,28},{24,16},{28,20},{1,9},{5... | collective-permute-start | bytes 442376 | tf_op jit(solution)/shard_map/ppermute | solution.py:26
  68.4 38.9 %collective-permute-start.21 = (bf16[512,512]{1,0:T(8,128)(2,1)S(1)}, bf16[512,512]{1,0:T(8,128)(2,1)S(1)}, u32[]{:S(2)}, u32[]{:S(2)}) collective-permute-start(bf16[512,512]{1,0:T(8,128)(2,1)S(1)} %get-tuple-element.72.refs_0_), channel_id=1, source_target_pairs={{0,8},{4,12},{8,0},{12,4},{16,24},{20,28},{24,16},{28,20},{1,9},{5... | collective-permute-start | bytes 1572872 | tf_op jit(solution)/shard_map/ppermute | solution.py:26
  73.3 2.8 %collective-permute-start.13 = (bf16[256,512]{1,0:T(8,128)(2,1)S(1)}, bf16[256,512]{1,0:T(8,128)(2,1)S(1)}, u32[]{:S(2)}, u32[]{:S(2)}) collective-permute-start(bf16[256,512]{1,0:T(8,128)(2,1)S(1)} %get-tuple-element.62), channel_id=1, source_target_pairs={{0,1},{1,0},{2,3},{3,2},{4,5},{5,4},{6,7},{7,6},{8,9},{9,8},{10,11... | collective-permute-start | bytes 786440 | tf_op jit(solution)/shard_map/ppermute | solution.py:26
  73.4 17.2 %collective-permute-start.14 = (bf16[256,512]{1,0:T(8,128)(2,1)S(1)}, bf16[256,512]{1,0:T(8,128)(2,1)S(1)}, u32[]{:S(2)}, u32[]{:S(2)}) collective-permute-start(bf16[256,512]{1,0:T(8,128)(2,1)S(1)} %get-tuple-element.63), channel_id=1, source_target_pairs={{0,2},{1,3},{2,0},{3,1},{4,6},{5,7},{6,4},{7,5},{8,10},{9,11},{10,... | collective-permute-start | bytes 786440 | tf_op jit(solution)/shard_map/ppermute | solution.py:26
  75.0 12.1 %collective-permute-start.20 = (bf16[144,512]{1,0:T(8,128)(2,1)S(1)}, bf16[144,512]{1,0:T(8,128)(2,1)S(1)}, u32[]{:S(2)}, u32[]{:S(2)}) collective-permute-start(bf16[144,512]{1,0:T(8,128)(2,1)S(1)} %get-tuple-element.71), channel_id=1, source_target_pairs={{0,16},{4,20},{8,24},{12,28},{16,0},{20,4},{24,8},{28,12},{1,17},{... | collective-permute-start | bytes 442376 | tf_op jit(solution)/shard_map/ppermute | solution.py:26
  76.2 14.5 %collective-permute-start.15 = (bf16[256,512]{1,0:T(8,128)(2,1)S(1)}, bf16[256,512]{1,0:T(8,128)(2,1)S(1)}, u32[]{:S(2)}, u32[]{:S(2)}) collective-permute-start(bf16[256,512]{1,0:T(8,128)(2,1)S(1)} %get-tuple-element.64), channel_id=1, source_target_pairs={{0,3},{1,2},{2,1},{3,0},{4,7},{5,6},{6,5},{7,4},{8,11},{9,10},{10,... | collective-permute-start | bytes 786440 | tf_op jit(solution)/shard_map/ppermute | solution.py:26
  76.2 33.6 %collective-permute-start.16 = (bf16[256,512]{1,0:T(8,128)(2,1)S(1)}, bf16[256,512]{1,0:T(8,128)(2,1)S(1)}, u32[]{:S(2)}, u32[]{:S(2)}) collective-permute-start(bf16[256,512]{1,0:T(8,128)(2,1)S(1)} %copy-done.5), channel_id=1, source_target_pairs={{0,16},{4,20},{8,24},{12,28},{16,0},{20,4},{24,8},{28,12},{1,17},{... | collective-permute-start | bytes 786440 | tf_op jit(solution)/shard_map/ppermute | solution.py:26
  87.1 22.7 %collective-permute-start.17 = (bf16[256,512]{1,0:T(8,128)(2,1)S(1)}, bf16[256,512]{1,0:T(8,128)(2,1)S(1)}, u32[]{:S(2)}, u32[]{:S(2)}) collective-permute-start(bf16[256,512]{1,0:T(8,128)(2,1)S(1)} %get-tuple-element.44.grad), channel_id=1, source_target_pairs={{0,16},{4,20},{8,24},{12,28},{16,0},{20,4},{24,8},{28,12},{1,17},{... | collective-permute-start | bytes 786440 | tf_op jit(solution)/shard_map/ppermute | solution.py:26
  90.6 9.3 %collective-permute-start.23 = (bf16[128,512]{1,0:T(8,128)(2,1)S(1)}, bf16[128,512]{1,0:T(8,128)(2,1)S(1)}, u32[]{:S(2)}, u32[]{:S(2)}) collective-permute-start(bf16[128,512]{1,0:T(8,128)(2,1)S(1)} %shard_map.119.refs_0_), channel_id=1, source_target_pairs={{0,8},{4,12},{8,0},{12,4},{16,24},{20,28},{24,16},{28,20},{1,9},{5... | collective-permute-start | bytes 393224 | tf_op jit(solution)/shard_map/ppermute | solution.py:26
  90.7 21.7 %collective-permute-start.24 = (bf16[128,512]{1,0:T(8,128)(2,1)S(1)}, bf16[128,512]{1,0:T(8,128)(2,1)S(1)}, u32[]{:S(2)}, u32[]{:S(2)}) collective-permute-start(bf16[128,512]{1,0:T(8,128)(2,1)S(1)} %shard_map.119.refs_0_), channel_id=1, source_target_pairs={{0,4},{4,0},{8,12},{12,8},{16,20},{20,16},{24,28},{28,24},{1,5},{5... | collective-permute-start | bytes 393224 | tf_op jit(solution)/shard_map/ppermute | solution.py:26
  99.9 12.5 %collective-permute-start.25 = (bf16[128,512]{1,0:T(8,128)(2,1)S(1)}, bf16[128,512]{1,0:T(8,128)(2,1)S(1)}, u32[]{:S(2)}, u32[]{:S(2)}) collective-permute-start(bf16[128,512]{1,0:T(8,128)(2,1)S(1)} %collective-permute-done.23.refs_1_), channel_id=1, source_target_pairs={{0,4},{4,0},{8,12},{12,8},{16,20},{20,16},{24,28},{28,24},{1,5},{5... | collective-permute-start | bytes 393224 | tf_op jit(solution)/shard_map/ppermute | solution.py:26
where the time goes:
time: 114 us
  waiting for transfers between devices  55.9 us (49%)
  starting transfers between devices  31.1 us (27%)
  Pallas kernels  23.2 us (20%)
  local copies, waits for them, and re-layouts  2.61 us (2%)
    ppermute x26, waiting for transfers between devices, swap(): lax.ppermute(shard, axis, [(i, i ^ mask) for i in range(lax.axis_size(axi...  55.9 us
    ppermute x26, starting transfers between devices, swap(): lax.ppermute(shard, axis, [(i, i ^ mask) for i in range(lax.axis_size(axi...  31.1 us
    pallas_call x19, Pallas kernels, call(): pl.pallas_call(kernel, in_specs=in_specs, out_specs=outs, out_shape=out_s...  23.2 us
    unnamed x18, local copies, waits for them, and re-layouts  2.61 us
  transfers between devices with their start and end apart: 26, of which 11 were waited for; matrix products, arithmetic and copies ran while one was open for 0% of the time, Pallas kernels for 19%

commit v1 on v0

--- a/solution.py
+++ b/solution.py
@@ -26,9 +26,9 @@
     return lax.ppermute(shard, axis, [(i, i ^ mask) for i in range(lax.axis_size(axis))])
 
 
-def call(kernel, out_shape, *operands, scalars=0, scratch=()):
+def call(kernel, out_shape, *operands, scalars=0, scratch=(), outside=()):
     in_specs = [pl.BlockSpec(memory_space=pltpu.SMEM)] * scalars
-    in_specs += [pl.BlockSpec(memory_space=pltpu.VMEM)] * (len(operands) - scalars)
+    in_specs += [pl.BlockSpec(memory_space=pltpu.VMEM)] * (len(operands) - scalars + len(outside))
     outs = [pl.BlockSpec(memory_space=pltpu.VMEM)] * len(out_shape)
     placed = [pltpu.with_memory_space_constraint(o, pltpu.VMEM) for o in operands[scalars:]]
     return pl.pallas_call(
@@ -38,7 +38,7 @@
         out_shape=out_shape,
         scratch_shapes=scratch,
         compiler_params=pltpu.CompilerParams(vmem_limit_bytes=KERNEL_VMEM),
-    )(*operands[:scalars], *placed)
+    )(*operands[:scalars], *placed, *outside)
 
 
 def like(shape, dtype=jnp.bfloat16):
@@ -80,7 +80,9 @@
         out[...] = dot(att_ref[...], weight_ref[:, pl.ds(start, width)]).astype(out.dtype)
 
 
-def hot_kernel(masks, groups, cols_ref, scatter_ref, *outs):
+def hot_kernel(masks, groups, cols_ref, key, value, key_copy, value_copy, scatter_ref, *outs):
+    key_copy[...] = key[...]
+    value_copy[...] = value[...]
     rows, slots = scatter_ref.shape
     device = lax.axis_index("ctx")
     row_ids = lax.broadcasted_iota(jnp.int32, (rows, slots), 0)
@@ -225,7 +227,8 @@
 
 def glob_kernel(parts, query, grad, near_stats, weights_in, value_term, *refs):
     values_in, owned = refs[:parts], refs[parts : 2 * parts - 1]
-    keep_out, send_out, delta_out, score_out, value_out, stats = refs[2 * parts - 1 :]
+    keep_on, keep_out, send_on, send_out, delta_out, score_out, value_out, stats = refs[2 * parts - 1 :]
+    half, upper = keep_out.shape[0], bit_of(2)
     heads, slots = query.shape[1] // HEAD_SIZE, value_out.shape[0]
     odd = jnp.bitwise_and(lax.axis_index("ctx"), 1) == 1
     every = pl.ds(0, query.shape[0])
@@ -242,8 +245,12 @@
         score_grad = (weights * (prob_grad - delta)).astype(BF16)
         score_out[:, glob] = score_grad
         key_term = dot(score_grad, query[:, part], TN)
-        keep_out[:, part] = jnp.where(odd, value_term[:, part], key_term)
-        send_out[:slots, part] = jnp.where(odd, key_term, value_term[:, part]).astype(BF16)
+        keep = jnp.where(odd, value_term[:, part], key_term)
+        send = jnp.where(odd, key_term, value_term[:, part])
+        keep_on[:, part] = jnp.where(upper, keep[:half], keep[half:])
+        keep_out[:, part] = jnp.where(upper, keep[half:], keep[:half])
+        send_on[:, part] = jnp.where(upper, send[:half], send[half:]).astype(BF16)
+        send_out[:half, part] = jnp.where(upper, send[half:], send[:half]).astype(BF16)
         notes = (top, *thirds(scale), *thirds(delta))
         put_columns(stats, every, head, notes, step=heads, width=1)
         put_columns(delta_out, every, head, (delta,))
@@ -254,7 +261,7 @@
         turned = stats[pl.ds(start, BLOCK), :].T
         for group in range(groups):
             at = pl.ds(group * query.shape[0] + start, BLOCK)
-            send_out[slots:, at] = turned[group * lines : (group + 1) * lines].astype(BF16)
+            send_out[half:, at] = turned[group * lines : (group + 1) * lines].astype(BF16)
 
 
 def rest_kernel(strides, cols_ref, weights_in, probs, deltas, glob_weights, scores_in, *refs):
@@ -347,28 +354,18 @@
     return jnp.bitwise_and(lax.axis_index("ctx"), mask) != 0
 
 
-def add_kernel(cut, last, total, got, mine, *outs):
-    slots = total.shape[0]
-    result = total[...] + got[:slots, :].astype(F32)
-    send = result
-    if cut:
-        low, high, upper = result[: slots // 2], result[slots // 2 :], bit_of(cut)
-        result, send = jnp.where(upper, high, low), jnp.where(upper, low, high)
-    if last:
-        outs[0][...] = result.astype(BF16)
-    else:
-        outs[0][...] = result
-        outs[1][: send.shape[0], :] = send.astype(BF16)
-        outs[1][send.shape[0] :, :] = mine[mine.shape[0] - outs[1].shape[0] + send.shape[0] :, :]
-
-
-def add(total, got, mine, notes, cut=0, last=False):
-    slots, width = total.shape
-    slots = slots // 2 if cut else slots
-    shapes = [like((slots, width))]
-    if not last:
-        shapes = [like((slots, width), F32), like((slots + notes, width))]
-    return call(functools.partial(add_kernel, cut, last), shapes, total, got, mine)
+def add_kernel(count, *refs):
+    parts, mine, outs = refs[:count], refs[count], refs[count + 1 :]
+    rows = parts[0].shape[0]
+    result = sum((part[:rows, :].astype(F32) for part in parts[1:]), parts[0][...])
+    for out in outs:
+        out[:rows, :] = result.astype(out.dtype)
+        if out.shape[0] > rows:
+            out[rows:, :] = mine[rows:, :]
+
+
+def add(parts, mine, *shapes):
+    return call(functools.partial(add_kernel, len(parts)), list(shapes), *parts, mine)
 
 
 def out_kernel(*refs):
@@ -411,16 +408,18 @@
     held = (0, *masks) if cube else (0,)
     owners = ((3, 5), (6, 7)) if cube else ()
 
-    scatter, *hot = call(
+    own_key, own_value, scatter, *hot = call(
         functools.partial(hot_kernel, held, owners),
-        [like((rows, slots))]
+        [like((rows, width))] * 2
+        + [like((rows, slots))]
         + [like((slots, rows))] * len(held)
         + [like((slots, HEAD_SIZE), F32)] * len(owners),
         global_cols.reshape(1, -1),
+        outside=(key_act, value_act),
     )
     selects, owned = hot[: len(held)], hot[len(held) :]
-    near_keys = [key_act] + [swap(key_act, "ctx", m) for m in masks]
-    near_values = [value_act] + [swap(value_act, "ctx", m) for m in masks]
+    near_keys = [own_key] + [swap(key_act, "ctx", m) for m in masks]
+    near_values = [own_value] + [swap(value_act, "ctx", m) for m in masks]
     pieces = [cotangent] + [swap(cotangent, "head", m) for m in range(1, groups)]
     if cube:
         glob = []
@@ -430,7 +429,7 @@
             glob.append([have, swap(have, "ctx", 2)])
         glob_keys, glob_values = glob
     else:
-        parts = (select_globals(selects, [key_act]), select_globals(selects, [value_act]))
+        parts = (select_globals(selects, [own_key]), select_globals(selects, [own_value]))
         glob_keys, glob_values = ([part] for part in lax.psum(parts, "ctx"))
     attn_grad, pair = call(
         grad_kernel, [like((rows, width)), like((2 * rows, width))], out_weight, query_act, *pieces
@@ -438,7 +437,7 @@
     pairs = [[pair]] + [[swap(pair, "ctx", m)] for m in masks[:-1]]
     m = masks[-1]
     pairs.append([swap(query_act, "ctx", m), swap(attn_grad, "ctx", m)])
-    near_all = [key_act, value_act, *near_keys[1:], *near_values[1:]]
+    near_all = [own_key, own_value, *near_keys[1:], *near_values[1:]]
     heads = width // HEAD_SIZE
     near = (strides + 1) * BLOCK
     weights, probs, glob_weights, value_term, glob_key, near_stats = call(
@@ -459,11 +458,14 @@
         *owned[1:],
         scalars=1,
     )
-    total, message, deltas, scores, glob_value = call(
+    notes = note_lines(rows, width)[1]
+    keep_on, keep, send_on, message, deltas, scores, glob_value = call(
         functools.partial(glob_kernel, len(glob_values)),
         [
-            like((slots, width), F32),
-            like((slots + note_lines(rows, width)[1], width)),
+            like((slots // 2, width), F32),
+            like((slots // 2, width), F32),
+            like((slots // 2, width)),
+            like((slots // 2 + notes, width)),
             like((rows, BLOCK), F32),
             like((rows, heads * slots)),
             like((slots, width)),
@@ -493,23 +495,33 @@
     )
     messages = [message]
     if cube:
-        notes = note_lines(rows, width)[1]
+        half = (slots // 2, width)
+        came = swap(send_on, "ctx", 1)
         messages.append(swap(message, "ctx", 1))
-        total, message = add(total, messages[1], messages[0], notes, cut=2)
+        (message,) = add([keep_on, came], messages[0], like(messages[0].shape))
         messages.append(swap(message, "ctx", 2))
-        total, message = add(total, messages[2], messages[0], notes)
+        total, message = add(
+            [keep, *messages[1:]], messages[0], like(half, F32), like(messages[0].shape)
+        )
         messages.append(swap(message, "ctx", 4))
-        (mine,) = add(total, messages[3], messages[0], notes, last=True)
+        (mine,) = add([total, messages[3]], messages[0], like(half))
         other = swap(mine, "ctx", 2)
         kept = [mine, other]
         got = [swap(mine, "ctx", 1), swap(other, "ctx", 1)]
     else:
         messages += [swap(message, "ctx", m) for m in masks]
-        odd = jnp.bitwise_and(lax.axis_index("ctx"), 1) == 1
-        send = message[:slots].astype(F32)
-        key_term, value_term = lax.psum(
-            (jnp.where(odd, send, total), jnp.where(odd, total, send)), "ctx"
+        odd, upper = (jnp.bitwise_and(lax.axis_index("ctx"), mask) != 0 for mask in (1, 2))
+        sends = send_on.astype(F32), message[: slots // 2].astype(F32)
+        halves = []
+        for keep_half, send_half in zip((keep_on, keep), sends):
+            halves.append(
+                (jnp.where(odd, send_half, keep_half), jnp.where(odd, keep_half, send_half))
+            )
+        ordered = tuple(
+            jnp.concatenate([jnp.where(upper, on, out), jnp.where(upper, out, on)], 0)
+            for on, out in zip(*halves)
         )
+        key_term, value_term = lax.psum(ordered, "ctx")
         kept = [jnp.where(odd, value_term, key_term).astype(BF16)]
         got = [jnp.where(odd, key_term, value_term).astype(BF16)]
     term = out_weight.shape[1] // groups
@@ -520,7 +532,7 @@
     layer_out = call(out_kernel, [out_shape], terms[0], *parts)[0]
     so_far = ()
     for at, m in enumerate([0, *masks]):
-        so_far = key_side(at - 1, cols, key_act, value_act, pairs[at], messages[at], so_far)
+        so_far = key_side(at - 1, cols, own_key, own_value, pairs[at], messages[at], so_far)
     key_sum, value_sum = so_far
     key_grad, value_grad = finish(2, scatter, key_sum, value_sum, kept, got)
     return (layer_out, query_grad, key_grad, value_grad)

time: 114 us -> 110 us (0.965)
  waiting for transfers between devices: 55.9 us -> 50.2 us
  starting transfers between devices: 31.1 us -> 32.6 us
    ppermute x26 -> x27, waiting for transfers between devices: 55.9 us -> 50.2 us  [swap(): lax.ppermute(shard, axis, [(i, i ^ mask) for i in range(lax.axis_size(axi...]
    ppermute x26 -> x27, starting transfers between devices: 31.1 us -> 32.6 us  [swap(): lax.ppermute(shard, axis, [(i, i ^ mask) for i in range(lax.axis_size(axi...]
    unnamed x18 -> x14, local copies, waits for them, and re-layouts: 2.61 us -> 2.6 us
  transfers between devices with their start and end apart: 26 -> 27, of which waited for: 11 -> 11; matrix products, arithmetic and copies ran while one was open for 0% -> 0% of each run, Pallas kernels for 19% -> 20%
where the time goes in v1:
time: 110 us; the launch traced here: 109 us
  waiting for transfers between devices  50.2 us (46%)
  starting transfers between devices  32.6 us (30%)
  Pallas kernels  23.2 us (21%)
  local copies, waits for them, and re-layouts  2.6 us (2%)
    ppermute x27, waiting for transfers between devices, swap(): lax.ppermute(shard, axis, [(i, i ^ mask) for i in range(lax.axis_size(axi...  50.2 us
    ppermute x27, starting transfers between devices, swap(): lax.ppermute(shard, axis, [(i, i ^ mask) for i in range(lax.axis_size(axi...  32.6 us
    pallas_call x19, Pallas kernels, call(): pl.pallas_call(kernel, in_specs=in_specs, out_specs=outs, out_shape=out_s...  23.2 us
    unnamed x14, local copies, waits for them, and re-layouts  2.6 us
  transfers between devices with their start and end apart: 27, of which 11 were waited for; matrix products, arithmetic and copies ran while one was open for 0% of the time, Pallas kernels for 20%

profile of v1, /device:TPU:0, one launch (start us, length us, event | category | flops | bytes accessed | tf_op | source)
XLA Modules:
  0.0 109.5 jit_solution(12947143039219428445)
XLA Ops:
  0.6 3.1 %collective-permute-start.3 = (bf16[256,512]{1,0:T(8,128)(2,1)}, bf16[256,512]{1,0:T(8,128)(2,1)S(1)}, u32[]{:S(2)}, u32[]{:S(2)}) collective-permute-start(bf16[256,512]{1,0:T(8,128)(2,1)} %key.1), channel_id=1, source_target_pairs={{0,4},{4,0},{8,12},{12,8},{16,20},{20,16},{24,28},{28,24},{1,5},{5... | collective-permute-start | bytes 786440 | tf_op jit(solution)/shard_map/ppermute | solution.py:26
  3.7 1.6 %collective-permute-start.4 = (bf16[256,512]{1,0:T(8,128)(2,1)}, bf16[256,512]{1,0:T(8,128)(2,1)S(1)}, u32[]{:S(2)}, u32[]{:S(2)}) collective-permute-start(bf16[256,512]{1,0:T(8,128)(2,1)} %key.1), channel_id=1, source_target_pairs={{0,8},{4,12},{8,0},{12,4},{16,24},{20,28},{24,16},{28,20},{1,9},{5... | collective-permute-start | bytes 786440 | tf_op jit(solution)/shard_map/ppermute | solution.py:26
  5.3 2.6 %collective-permute-start.5 = (bf16[256,512]{1,0:T(8,128)(2,1)}, bf16[256,512]{1,0:T(8,128)(2,1)S(1)}, u32[]{:S(2)}, u32[]{:S(2)}) collective-permute-start(bf16[256,512]{1,0:T(8,128)(2,1)} %key.1), channel_id=1, source_target_pairs={{0,16},{4,20},{8,24},{12,28},{16,0},{20,4},{24,8},{28,12},{1,17},{... | collective-permute-start | bytes 786440 | tf_op jit(solution)/shard_map/ppermute | solution.py:26
  7.9 0.5 collective-permute-start.6
  8.4 0.4 collective-permute-start.7
  8.8 1.9 %collective-permute-done.3.refs_5_.refs_2_.refs_4_ = bf16[256,512]{1,0:T(8,128)(2,1)S(1)} collective-permute-done((bf16[256,512]{1,0:T(8,128)(2,1)}, bf16[256,512]{1,0:T(8,128)(2,1)S(1)}, u32[]{:S(2)}, u32[]{:S(2)}) %collective-permute-start.3) | collective-permute-done | bytes 262176 | tf_op jit(solution)/shard_map/ppermute | solution.py:26
  10.8 3.4 %collective-permute-start.8 = (bf16[256,512]{1,0:T(8,128)(2,1)}, bf16[256,512]{1,0:T(8,128)(2,1)S(1)}, u32[]{:S(2)}, u32[]{:S(2)}) collective-permute-start(bf16[256,512]{1,0:T(8,128)(2,1)} %value.1), channel_id=1, source_target_pairs={{0,16},{4,20},{8,24},{12,28},{16,0},{20,4},{24,8},{28,12},{1,17},{... | collective-permute-start | bytes 786440 | tf_op jit(solution)/shard_map/ppermute | solution.py:26
  14.2 0.9 copy-done.2
  15.1 0.9 copy-done.3
  16.1 0.7 copy-done.6
  17.0 2.1 %collective-permute-done.4.refs_6_.refs_3_.refs_5_ = bf16[256,512]{1,0:T(8,128)(2,1)S(1)} collective-permute-done((bf16[256,512]{1,0:T(8,128)(2,1)}, bf16[256,512]{1,0:T(8,128)(2,1)S(1)}, u32[]{:S(2)}, u32[]{:S(2)}) %collective-permute-start.4) | collective-permute-done | bytes 262176 | tf_op jit(solution)/shard_map/ppermute | solution.py:26
  19.1 1.7 %collective-permute-done.5.refs_7_.refs_4_.refs_6_ = bf16[256,512]{1,0:T(8,128)(2,1)S(1)} collective-permute-done((bf16[256,512]{1,0:T(8,128)(2,1)}, bf16[256,512]{1,0:T(8,128)(2,1)S(1)}, u32[]{:S(2)}, u32[]{:S(2)}) %collective-permute-start.5) | collective-permute-done | bytes 262176 | tf_op jit(solution)/shard_map/ppermute | solution.py:26
  20.7 0.4 shard_map.104.have
  21.3 7.1 %collective-permute-done.7.refs_6_.refs_8_ = bf16[256,512]{1,0:T(8,128)(2,1)S(1)} collective-permute-done((bf16[256,512]{1,0:T(8,128)(2,1)}, bf16[256,512]{1,0:T(8,128)(2,1)S(1)}, u32[]{:S(2)}, u32[]{:S(2)}) %collective-permute-start.7) | collective-permute-done | bytes 262176 | tf_op jit(solution)/shard_map/ppermute | solution.py:26
  28.4 2.4 %collective-permute-done.8.refs_7_.refs_9_ = bf16[256,512]{1,0:T(8,128)(2,1)S(1)} collective-permute-done((bf16[256,512]{1,0:T(8,128)(2,1)}, bf16[256,512]{1,0:T(8,128)(2,1)S(1)}, u32[]{:S(2)}, u32[]{:S(2)}) %collective-permute-start.8) | collective-permute-done | bytes 262176 | tf_op jit(solution)/shard_map/ppermute | solution.py:26
  30.8 0.4 shard_map.107.have
  31.3 0.6 collective-permute-start.11
  31.8 1.5 %collective-permute-start.1 = (bf16[256,512]{1,0:T(8,128)(2,1)S(1)}, bf16[256,512]{1,0:T(8,128)(2,1)S(1)}, u32[]{:S(2)}, u32[]{:S(2)}) collective-permute-start(bf16[256,512]{1,0:T(8,128)(2,1)S(1)} %copy-done.4), channel_id=1, source_target_pairs={{0,2},{1,3},{2,0},{3,1},{4,6},{5,7},{6,4},{7,5},{8,10},{9,11},{10,... | collective-permute-start | bytes 786440 | tf_op jit(solution)/shard_map/ppermute | solution.py:26
  33.8 0.5 collective-permute-start.10
  34.3 3.4 %collective-permute-done.11.got = bf16[256,512]{1,0:T(8,128)(2,1)S(1)} collective-permute-done((bf16[256,512]{1,0:T(8,128)(2,1)S(1)}, bf16[256,512]{1,0:T(8,128)(2,1)S(1)}, u32[]{:S(2)}, u32[]{:S(2)}) %collective-permute-start.11) | collective-permute-done | bytes 262176 | tf_op jit(solution)/shard_map/ppermute | solution.py:26
  37.8 1.0 collective-permute-start.12
  38.8 2.2 %collective-permute-done.1.refs_2_ = bf16[256,512]{1,0:T(8,128)(2,1)S(1)} collective-permute-done((bf16[256,512]{1,0:T(8,128)(2,1)S(1)}, bf16[256,512]{1,0:T(8,128)(2,1)S(1)}, u32[]{:S(2)}, u32[]{:S(2)}) %collective-permute-start.1) | collective-permute-done | bytes 262176 | tf_op jit(solution)/shard_map/ppermute | solution.py:26
  41.0 4.7 %collective-permute-done.2.refs_3_ = bf16[256,512]{1,0:T(8,128)(2,1)S(1)} collective-permute-done((bf16[256,512]{1,0:T(8,128)(2,1)S(1)}, bf16[256,512]{1,0:T(8,128)(2,1)S(1)}, u32[]{:S(2)}, u32[]{:S(2)}) %collective-permute-start.2) | collective-permute-done | bytes 262176 | tf_op jit(solution)/shard_map/ppermute | solution.py:26
  45.7 0.7 shard_map.102
  46.5 1.6 %collective-permute-start.23 = (bf16[512,512]{1,0:T(8,128)(2,1)S(1)}, bf16[512,512]{1,0:T(8,128)(2,1)S(1)}, u32[]{:S(2)}, u32[]{:S(2)}) collective-permute-start(bf16[512,512]{1,0:T(8,128)(2,1)S(1)} %get-tuple-element.76.refs_0_), channel_id=1, source_target_pairs={{0,4},{4,0},{8,12},{12,8},{16,20},{20,16},{24,28},{28,24},{1,5},{5... | collective-permute-start | bytes 1572872 | tf_op jit(solution)/shard_map/ppermute | solution.py:26
  48.1 3.5 %shard_map.106 = (f32[256,2048]{1,0:T(8,128)S(1)}, f32[256,2048]{1,0:T(8,128)S(1)}, f32[256,1024]{1,0:T(8,128)S(1)}, f32[256,512]{1,0:T(8,128)S(1)}, bf16[256,51...) custom-call(s32[3,16]{1,0:T(4,128)S(1)} %bitcast.2, bf16[256,512]{1,0:T(8,128)(2,1)S(1)} %copy-done.1, ...), custom_call_target="tpu_custom_call" | custom-call | tf_op jit(solution)/shard_map/pallas_call | solution.py:34
  51.6 2.1 %shard_map.109 = (f32[128,512]{1,0:T(8,128)S(1)}, f32[128,512]{1,0:T(8,128)S(1)}, bf16[128,512]{1,0:T(8,128)(2,1)S(1)}, bf16[144,512]{1,0:T(8,128)(2,1)S(1)}, f3...) custom-call(bf16[256,512]{1,0:T(8,128)(2,1)S(1)} %copy-done.1, ...), custom_call_target="tpu_custom_call" | custom-call | tf_op jit(solution)/shard_map/pallas_call | solution.py:34
  53.6 0.5 collective-permute-start.19
  54.2 1.5 %collective-permute-start.18 = (bf16[144,512]{1,0:T(8,128)(2,1)S(1)}, bf16[144,512]{1,0:T(8,128)(2,1)S(1)}, u32[]{:S(2)}, u32[]{:S(2)}) collective-permute-start(bf16[144,512]{1,0:T(8,128)(2,1)S(1)} %get-tuple-element.72.refs_2_.refs_3_.refs_1_), channel_id=1, source_target_pairs={{0,4},{4,0},{8,12},{12,8},{16,20},{20,16},{24,28},{28,24},{1,5},{5... | collective-permute-start | bytes 442376 | tf_op jit(solution)/shard_map/ppermute | solution.py:26
  55.7 8.4 %collective-permute-done.19.refs_1_ = bf16[128,512]{1,0:T(8,128)(2,1)S(1)} collective-permute-done((bf16[128,512]{1,0:T(8,128)(2,1)S(1)}, bf16[128,512]{1,0:T(8,128)(2,1)S(1)}, u32[]{:S(2)}, u32[]{:S(2)}) %collective-permute-start.19) | collective-permute-done | bytes 131104 | tf_op jit(solution)/shard_map/ppermute | solution.py:26
  64.2 0.5 collective-permute-start.20
  64.7 1.6 %collective-permute-start.22 = (bf16[512,512]{1,0:T(8,128)(2,1)S(1)}, bf16[512,512]{1,0:T(8,128)(2,1)S(1)}, u32[]{:S(2)}, u32[]{:S(2)}) collective-permute-start(bf16[512,512]{1,0:T(8,128)(2,1)S(1)} %get-tuple-element.76.refs_0_), channel_id=1, source_target_pairs={{0,8},{4,12},{8,0},{12,4},{16,24},{20,28},{24,16},{28,20},{1,9},{5... | collective-permute-start | bytes 1572872 | tf_op jit(solution)/shard_map/ppermute | solution.py:26
  66.3 2.6 %shard_map.110 = (bf16[256,512]{1,0:T(8,128)(2,1)S(1)}, bf16[256,512]{1,0:T(8,128)(2,1)}) custom-call(s32[3,16]{1,0:T(4,128)S(1)} %bitcast.3, f32[256,2048]{1,0:T(8,128)S(1)} %get-tuple-element.55.weights_in, f32[256,2048]{1,0:T(8,128)S(1)} %get-tuple-element.56.probs, f32[256,128]{1,0:T(8,128)S(1)} %get-tuple-element.60.deltas, ...), custom_call_target="tpu_custom_call" | custom-call | tf_op jit(solution)/shard_map/pallas_call | solution.py:34
  68.8 0.7 shard_map.111
  69.7 1.6 %collective-permute-start.14 = (bf16[256,512]{1,0:T(8,128)(2,1)S(1)}, bf16[256,512]{1,0:T(8,128)(2,1)S(1)}, u32[]{:S(2)}, u32[]{:S(2)}) collective-permute-start(bf16[256,512]{1,0:T(8,128)(2,1)S(1)} %get-tuple-element.67), channel_id=1, source_target_pairs={{0,2},{1,3},{2,0},{3,1},{4,6},{5,7},{6,4},{7,5},{8,10},{9,11},{10,... | collective-permute-start | bytes 786440 | tf_op jit(solution)/shard_map/ppermute | solution.py:26
  71.3 1.1 %collective-permute-start.21 = (bf16[144,512]{1,0:T(8,128)(2,1)S(1)}, bf16[144,512]{1,0:T(8,128)(2,1)S(1)}, u32[]{:S(2)}, u32[]{:S(2)}) collective-permute-start(bf16[144,512]{1,0:T(8,128)(2,1)S(1)} %get-tuple-element.75), channel_id=1, source_target_pairs={{0,16},{4,20},{8,24},{12,28},{16,0},{20,4},{24,8},{28,12},{1,17},{... | collective-permute-start | bytes 442376 | tf_op jit(solution)/shard_map/ppermute | solution.py:26
  72.4 1.9 %collective-permute-start.16 = (bf16[256,512]{1,0:T(8,128)(2,1)S(1)}, bf16[256,512]{1,0:T(8,128)(2,1)S(1)}, u32[]{:S(2)}, u32[]{:S(2)}) collective-permute-start(bf16[256,512]{1,0:T(8,128)(2,1)S(1)} %copy-done.1), channel_id=1, source_target_pairs={{0,16},{4,20},{8,24},{12,28},{16,0},{20,4},{24,8},{28,12},{1,17},{... | collective-permute-start | bytes 786440 | tf_op jit(solution)/shard_map/ppermute | solution.py:26
  74.4 9.0 %collective-permute-done.21.refs_2_.refs_1_ = bf16[144,512]{1,0:T(8,128)(2,1)S(1)} collective-permute-done((bf16[144,512]{1,0:T(8,128)(2,1)S(1)}, bf16[144,512]{1,0:T(8,128)(2,1)S(1)}, u32[]{:S(2)}, u32[]{:S(2)}) %collective-permute-start.21) | collective-permute-done | bytes 147488 | tf_op jit(solution)/shard_map/ppermute | solution.py:26
  83.3 3.4 %collective-permute-start.17 = (bf16[256,512]{1,0:T(8,128)(2,1)S(1)}, bf16[256,512]{1,0:T(8,128)(2,1)S(1)}, u32[]{:S(2)}, u32[]{:S(2)}) collective-permute-start(bf16[256,512]{1,0:T(8,128)(2,1)S(1)} %get-tuple-element.46.grad), channel_id=1, source_target_pairs={{0,16},{4,20},{8,24},{12,28},{16,0},{20,4},{24,8},{28,12},{1,17},{... | collective-permute-start | bytes 786440 | tf_op jit(solution)/shard_map/ppermute | solution.py:26
  86.9 1.6 %collective-permute-start.25 = (bf16[128,512]{1,0:T(8,128)(2,1)S(1)}, bf16[128,512]{1,0:T(8,128)(2,1)S(1)}, u32[]{:S(2)}, u32[]{:S(2)}) collective-permute-start(bf16[128,512]{1,0:T(8,128)(2,1)S(1)} %shard_map.119.refs_0_), channel_id=1, source_target_pairs={{0,4},{4,0},{8,12},{12,8},{16,20},{20,16},{24,28},{28,24},{1,5},{5... | collective-permute-start | bytes 393224 | tf_op jit(solution)/shard_map/ppermute | solution.py:26
  88.5 7.3 %collective-permute-done.24.refs_1_ = bf16[128,512]{1,0:T(8,128)(2,1)S(1)} collective-permute-done((bf16[128,512]{1,0:T(8,128)(2,1)S(1)}, bf16[128,512]{1,0:T(8,128)(2,1)S(1)}, u32[]{:S(2)}, u32[]{:S(2)}) %collective-permute-start.24) | collective-permute-done | bytes 131104 | tf_op jit(solution)/shard_map/ppermute | solution.py:26
  95.8 1.5 %collective-permute-start.26 = (bf16[128,512]{1,0:T(8,128)(2,1)S(1)}, bf16[128,512]{1,0:T(8,128)(2,1)S(1)}, u32[]{:S(2)}, u32[]{:S(2)}) collective-permute-start(bf16[128,512]{1,0:T(8,128)(2,1)S(1)} %collective-permute-done.24.refs_1_), channel_id=1, source_target_pairs={{0,4},{4,0},{8,12},{12,8},{16,20},{20,16},{24,28},{28,24},{1,5},{5... | collective-permute-start | bytes 393224 | tf_op jit(solution)/shard_map/ppermute | solution.py:26
  97.3 2.5 %shard_map.115 = (f32[256,512]{1,0:T(8,128)S(1)}, f32[256,512]{1,0:T(8,128)S(1)}) custom-call(s32[3,16]{1,0:T(4,128)S(1)} %bitcast.4, bf16[256,512]{1,0:T(8,128)(2,1)S(1)} %get-tuple-element.47.refs_4_.refs_0_.refs_2_.key, bf16[256,512]{1,0:T(8,128)(2,1)S(1)} %get-tuple-element.48.refs_1_.refs_4_.refs_3_.value, ...), custom_call_target="tpu_custom_call" | custom-call | tf_op jit(solution)/shard_map/pallas_call | solution.py:34
  99.8 2.5 %shard_map.116 = (f32[256,512]{1,0:T(8,128)S(1)}, f32[256,512]{1,0:T(8,128)S(1)}) custom-call(s32[3,16]{1,0:T(4,128)S(1)} %bitcast.5, bf16[256,512]{1,0:T(8,128)(2,1)S(1)} %get-tuple-element.47.refs_4_.refs_0_.refs_2_.key, bf16[256,512]{1,0:T(8,128)(2,1)S(1)} %get-tuple-element.48.refs_1_.refs_4_.refs_3_.value, ...), custom_call_target="tpu_custom_call" | custom-call | tf_op jit(solution)/shard_map/pallas_call | solution.py:34
  102.3 0.8 shard_map.112
  103.2 2.5 %shard_map.117 = (f32[256,512]{1,0:T(8,128)S(1)}, f32[256,512]{1,0:T(8,128)S(1)}) custom-call(s32[3,16]{1,0:T(4,128)S(1)} %bitcast.6, bf16[256,512]{1,0:T(8,128)(2,1)S(1)} %get-tuple-element.47.refs_4_.refs_0_.refs_2_.key, bf16[256,512]{1,0:T(8,128)(2,1)S(1)} %get-tuple-element.48.refs_1_.refs_4_.refs_3_.value, ...), custom_call_target="tpu_custom_call" | custom-call | tf_op jit(solution)/shard_map/pallas_call | solution.py:34
  105.7 2.5 %shard_map.118 = (f32[256,512]{1,0:T(8,128)S(1)}, f32[256,512]{1,0:T(8,128)S(1)}) custom-call(s32[3,16]{1,0:T(4,128)S(1)} %bitcast.7, bf16[256,512]{1,0:T(8,128)(2,1)S(1)} %get-tuple-element.47.refs_4_.refs_0_.refs_2_.key, bf16[256,512]{1,0:T(8,128)(2,1)S(1)} %get-tuple-element.48.refs_1_.refs_4_.refs_3_.value, ...), custom_call_target="tpu_custom_call" | custom-call | tf_op jit(solution)/shard_map/pallas_call | solution.py:34
  108.3 1.2 %shard_map.120 = (bf16[256,512]{1,0:T(8,128)(2,1)}, bf16[256,512]{1,0:T(8,128)(2,1)}) custom-call(bf16[256,256]{1,0:T(8,128)(2,1)S(1)} %get-tuple-element.70.scatter, f32[256,512]{1,0:T(8,128)S(1)} %get-tuple-element.83.key, f32[256,512]{1,0:T(8,128)S(1)} %get-tuple-element.84.value, bf16[128,512]{1,0:T(8,128)(2,1)S(1)} %shard_map.119.refs_0_, ...), custom_call_target="tpu_custom_call" | custom-call | tf_op jit(solution)/shard_map/pallas_call | solution.py:34
  (39 shorter events, 1.2 us)
Async XLA Ops:
  0.6 10.1 %collective-permute-start.3 = (bf16[256,512]{1,0:T(8,128)(2,1)}, bf16[256,512]{1,0:T(8,128)(2,1)S(1)}, u32[]{:S(2)}, u32[]{:S(2)}) collective-permute-start(bf16[256,512]{1,0:T(8,128)(2,1)} %key.1), channel_id=1, source_target_pairs={{0,4},{4,0},{8,12},{12,8},{16,20},{20,16},{24,28},{28,24},{1,5},{5... | collective-permute-start | bytes 786440 | tf_op jit(solution)/shard_map/ppermute | solution.py:26
  3.7 15.4 %collective-permute-start.4 = (bf16[256,512]{1,0:T(8,128)(2,1)}, bf16[256,512]{1,0:T(8,128)(2,1)S(1)}, u32[]{:S(2)}, u32[]{:S(2)}) collective-permute-start(bf16[256,512]{1,0:T(8,128)(2,1)} %key.1), channel_id=1, source_target_pairs={{0,8},{4,12},{8,0},{12,4},{16,24},{20,28},{24,16},{28,20},{1,9},{5... | collective-permute-start | bytes 786440 | tf_op jit(solution)/shard_map/ppermute | solution.py:26
  5.3 15.5 %collective-permute-start.5 = (bf16[256,512]{1,0:T(8,128)(2,1)}, bf16[256,512]{1,0:T(8,128)(2,1)S(1)}, u32[]{:S(2)}, u32[]{:S(2)}) collective-permute-start(bf16[256,512]{1,0:T(8,128)(2,1)} %key.1), channel_id=1, source_target_pairs={{0,16},{4,20},{8,24},{12,28},{16,0},{20,4},{24,8},{28,12},{1,17},{... | collective-permute-start | bytes 786440 | tf_op jit(solution)/shard_map/ppermute | solution.py:26
  7.9 13.4 %collective-permute-start.6 = (bf16[256,512]{1,0:T(8,128)(2,1)}, bf16[256,512]{1,0:T(8,128)(2,1)S(1)}, u32[]{:S(2)}, u32[]{:S(2)}) collective-permute-start(bf16[256,512]{1,0:T(8,128)(2,1)} %value.1), channel_id=1, source_target_pairs={{0,4},{4,0},{8,12},{12,8},{16,20},{20,16},{24,28},{28,24},{1,5},{5... | collective-permute-start | bytes 786440 | tf_op jit(solution)/shard_map/ppermute | solution.py:26
  8.4 20.0 %collective-permute-start.7 = (bf16[256,512]{1,0:T(8,128)(2,1)}, bf16[256,512]{1,0:T(8,128)(2,1)S(1)}, u32[]{:S(2)}, u32[]{:S(2)}) collective-permute-start(bf16[256,512]{1,0:T(8,128)(2,1)} %value.1), channel_id=1, source_target_pairs={{0,8},{4,12},{8,0},{12,4},{16,24},{20,28},{24,16},{28,20},{1,9},{5... | collective-permute-start | bytes 786440 | tf_op jit(solution)/shard_map/ppermute | solution.py:26
  10.8 20.1 %collective-permute-start.8 = (bf16[256,512]{1,0:T(8,128)(2,1)}, bf16[256,512]{1,0:T(8,128)(2,1)S(1)}, u32[]{:S(2)}, u32[]{:S(2)}) collective-permute-start(bf16[256,512]{1,0:T(8,128)(2,1)} %value.1), channel_id=1, source_target_pairs={{0,16},{4,20},{8,24},{12,28},{16,0},{20,4},{24,8},{28,12},{1,17},{... | collective-permute-start | bytes 786440 | tf_op jit(solution)/shard_map/ppermute | solution.py:26
  14.1 0.9 copy-start.2
  15.1 0.9 copy-start.3
  16.1 0.7 copy-start.6
  16.7 15.1 %copy-start.4 = (bf16[256,512]{1,0:T(8,128)(2,1)S(1)}, bf16[256,512]{1,0:T(8,128)(2,1)}, u32[]{:S(2)}) copy-start(bf16[256,512]{1,0:T(8,128)(2,1)} %refs_0_.1) | copy-start | bytes 786436
  21.2 24.6 %copy-start = (bf16[512,2048]{1,0:T(8,128)(2,1)S(1)}, bf16[512,2048]{1,0:T(8,128)(2,1)}, u32[]{:S(2)}) copy-start(bf16[512,2048]{1,0:T(8,128)(2,1)} %weight_ref.3) | copy-start | bytes 6291460
  21.2 24.5 %copy-start.1 = (bf16[256,512]{1,0:T(8,128)(2,1)S(1)}, bf16[256,512]{1,0:T(8,128)(2,1)}, u32[]{:S(2)}) copy-start(bf16[256,512]{1,0:T(8,128)(2,1)} %query.5) | copy-start | bytes 786436
  21.2 12.5 %collective-permute-start.9 = (bf16[256,512]{1,0:T(8,128)(2,1)S(1)}, bf16[256,512]{1,0:T(8,128)(2,1)S(1)}, u32[]{:S(2)}, u32[]{:S(2)}) collective-permute-start(bf16[256,512]{1,0:T(8,128)(2,1)S(1)} %shard_map.104.have), channel_id=1, source_target_pairs={{0,4},{4,0},{8,12},{12,8},{16,20},{20,16},{24,28},{28,24},{1,5},{5... | collective-permute-start | bytes 786440 | tf_op jit(solution)/shard_map/ppermute | solution.py:26
  31.3 6.4 %collective-permute-start.11 = (bf16[256,512]{1,0:T(8,128)(2,1)S(1)}, bf16[256,512]{1,0:T(8,128)(2,1)S(1)}, u32[]{:S(2)}, u32[]{:S(2)}) collective-permute-start(bf16[256,512]{1,0:T(8,128)(2,1)S(1)} %shard_map.107.have), channel_id=1, source_target_pairs={{0,4},{4,0},{8,12},{12,8},{16,20},{20,16},{24,28},{28,24},{1,5},{5... | collective-permute-start | bytes 786440 | tf_op jit(solution)/shard_map/ppermute | solution.py:26
  31.8 6.9 %collective-permute-start = (bf16[256,512]{1,0:T(8,128)(2,1)S(1)}, bf16[256,512]{1,0:T(8,128)(2,1)S(1)}, u32[]{:S(2)}, u32[]{:S(2)}) collective-permute-start(bf16[256,512]{1,0:T(8,128)(2,1)S(1)} %copy-done.4), channel_id=1, source_target_pairs={{0,1},{1,0},{2,3},{3,2},{4,5},{5,4},{6,7},{7,6},{8,9},{9,8},{10,11... | collective-permute-start | bytes 786440 | tf_op jit(solution)/shard_map/ppermute | solution.py:26
  31.8 9.2 %collective-permute-start.1 = (bf16[256,512]{1,0:T(8,128)(2,1)S(1)}, bf16[256,512]{1,0:T(8,128)(2,1)S(1)}, u32[]{:S(2)}, u32[]{:S(2)}) collective-permute-start(bf16[256,512]{1,0:T(8,128)(2,1)S(1)} %copy-done.4), channel_id=1, source_target_pairs={{0,2},{1,3},{2,0},{3,1},{4,6},{5,7},{6,4},{7,5},{8,10},{9,11},{10,... | collective-permute-start | bytes 786440 | tf_op jit(solution)/shard_map/ppermute | solution.py:26
  33.3 12.4 %collective-permute-start.2 = (bf16[256,512]{1,0:T(8,128)(2,1)S(1)}, bf16[256,512]{1,0:T(8,128)(2,1)S(1)}, u32[]{:S(2)}, u32[]{:S(2)}) collective-permute-start(bf16[256,512]{1,0:T(8,128)(2,1)S(1)} %copy-done.4), channel_id=1, source_target_pairs={{0,3},{1,2},{2,1},{3,0},{4,7},{5,6},{6,5},{7,4},{8,11},{9,10},{10,... | collective-permute-start | bytes 786440 | tf_op jit(solution)/shard_map/ppermute | solution.py:26
  33.8 14.3 %copy-start.5 = (s32[16,3]{0,1:T(4,128)S(1)}, s32[16,3]{0,1:T(4,128)}, u32[]{:S(2)}) copy-start(s32[16,3]{0,1:T(4,128)} %param.12) | copy-start | bytes 580
  33.8 14.2 %collective-permute-start.10 = (bf16[256,512]{1,0:T(8,128)(2,1)S(1)}, bf16[256,512]{1,0:T(8,128)(2,1)S(1)}, u32[]{:S(2)}, u32[]{:S(2)}) collective-permute-start(bf16[256,512]{1,0:T(8,128)(2,1)S(1)} %shard_map.105.refs_8_), channel_id=1, source_target_pairs={{0,8},{4,12},{8,0},{12,4},{16,24},{20,28},{24,16},{28,20},{1,9},{5... | collective-permute-start | bytes 786440 | tf_op jit(solution)/shard_map/ppermute | solution.py:26
  37.8 13.8 %collective-permute-start.12 = (bf16[256,512]{1,0:T(8,128)(2,1)S(1)}, bf16[256,512]{1,0:T(8,128)(2,1)S(1)}, u32[]{:S(2)}, u32[]{:S(2)}) collective-permute-start(bf16[256,512]{1,0:T(8,128)(2,1)S(1)} %shard_map.108.refs_0_), channel_id=1, source_target_pairs={{0,8},{4,12},{8,0},{12,4},{16,24},{20,28},{24,16},{28,20},{1,9},{5... | collective-permute-start | bytes 786440 | tf_op jit(solution)/shard_map/ppermute | solution.py:26
  46.5 26.0 %collective-permute-start.23 = (bf16[512,512]{1,0:T(8,128)(2,1)S(1)}, bf16[512,512]{1,0:T(8,128)(2,1)S(1)}, u32[]{:S(2)}, u32[]{:S(2)}) collective-permute-start(bf16[512,512]{1,0:T(8,128)(2,1)S(1)} %get-tuple-element.76.refs_0_), channel_id=1, source_target_pairs={{0,4},{4,0},{8,12},{12,8},{16,20},{20,16},{24,28},{28,24},{1,5},{5... | collective-permute-start | bytes 1572872 | tf_op jit(solution)/shard_map/ppermute | solution.py:26
  53.6 10.5 %collective-permute-start.19 = (bf16[128,512]{1,0:T(8,128)(2,1)S(1)}, bf16[128,512]{1,0:T(8,128)(2,1)S(1)}, u32[]{:S(2)}, u32[]{:S(2)}) collective-permute-start(bf16[128,512]{1,0:T(8,128)(2,1)S(1)} %get-tuple-element.74), channel_id=1, source_target_pairs={{0,4},{4,0},{8,12},{12,8},{16,20},{20,16},{24,28},{28,24},{1,5},{5... | collective-permute-start | bytes 393224 | tf_op jit(solution)/shard_map/ppermute | solution.py:26
  54.2 15.5 %collective-permute-start.18 = (bf16[144,512]{1,0:T(8,128)(2,1)S(1)}, bf16[144,512]{1,0:T(8,128)(2,1)S(1)}, u32[]{:S(2)}, u32[]{:S(2)}) collective-permute-start(bf16[144,512]{1,0:T(8,128)(2,1)S(1)} %get-tuple-element.72.refs_2_.refs_3_.refs_1_), channel_id=1, source_target_pairs={{0,4},{4,0},{8,12},{12,8},{16,20},{20,16},{24,28},{28,24},{1,5},{5... | collective-permute-start | bytes 442376 | tf_op jit(solution)/shard_map/ppermute | solution.py:26
  64.2 7.1 %collective-permute-start.20 = (bf16[144,512]{1,0:T(8,128)(2,1)S(1)}, bf16[144,512]{1,0:T(8,128)(2,1)S(1)}, u32[]{:S(2)}, u32[]{:S(2)}) collective-permute-start(bf16[144,512]{1,0:T(8,128)(2,1)S(1)} %shard_map.113), channel_id=1, source_target_pairs={{0,8},{4,12},{8,0},{12,4},{16,24},{20,28},{24,16},{28,20},{1,9},{5... | collective-permute-start | bytes 442376 | tf_op jit(solution)/shard_map/ppermute | solution.py:26
  64.7 38.5 %collective-permute-start.22 = (bf16[512,512]{1,0:T(8,128)(2,1)S(1)}, bf16[512,512]{1,0:T(8,128)(2,1)S(1)}, u32[]{:S(2)}, u32[]{:S(2)}) collective-permute-start(bf16[512,512]{1,0:T(8,128)(2,1)S(1)} %get-tuple-element.76.refs_0_), channel_id=1, source_target_pairs={{0,8},{4,12},{8,0},{12,4},{16,24},{20,28},{24,16},{28,20},{1,9},{5... | collective-permute-start | bytes 1572872 | tf_op jit(solution)/shard_map/ppermute | solution.py:26
  69.6 2.9 %collective-permute-start.13 = (bf16[256,512]{1,0:T(8,128)(2,1)S(1)}, bf16[256,512]{1,0:T(8,128)(2,1)S(1)}, u32[]{:S(2)}, u32[]{:S(2)}) collective-permute-start(bf16[256,512]{1,0:T(8,128)(2,1)S(1)} %get-tuple-element.66), channel_id=1, source_target_pairs={{0,1},{1,0},{2,3},{3,2},{4,5},{5,4},{6,7},{7,6},{8,9},{9,8},{10,11... | collective-permute-start | bytes 786440 | tf_op jit(solution)/shard_map/ppermute | solution.py:26
  69.7 17.1 %collective-permute-start.14 = (bf16[256,512]{1,0:T(8,128)(2,1)S(1)}, bf16[256,512]{1,0:T(8,128)(2,1)S(1)}, u32[]{:S(2)}, u32[]{:S(2)}) collective-permute-start(bf16[256,512]{1,0:T(8,128)(2,1)S(1)} %get-tuple-element.67), channel_id=1, source_target_pairs={{0,2},{1,3},{2,0},{3,1},{4,6},{5,7},{6,4},{7,5},{8,10},{9,11},{10,... | collective-permute-start | bytes 786440 | tf_op jit(solution)/shard_map/ppermute | solution.py:26
  71.3 12.1 %collective-permute-start.21 = (bf16[144,512]{1,0:T(8,128)(2,1)S(1)}, bf16[144,512]{1,0:T(8,128)(2,1)S(1)}, u32[]{:S(2)}, u32[]{:S(2)}) collective-permute-start(bf16[144,512]{1,0:T(8,128)(2,1)S(1)} %get-tuple-element.75), channel_id=1, source_target_pairs={{0,16},{4,20},{8,24},{12,28},{16,0},{20,4},{24,8},{28,12},{1,17},{... | collective-permute-start | bytes 442376 | tf_op jit(solution)/shard_map/ppermute | solution.py:26
  72.4 14.5 %collective-permute-start.15 = (bf16[256,512]{1,0:T(8,128)(2,1)S(1)}, bf16[256,512]{1,0:T(8,128)(2,1)S(1)}, u32[]{:S(2)}, u32[]{:S(2)}) collective-permute-start(bf16[256,512]{1,0:T(8,128)(2,1)S(1)} %get-tuple-element.68), channel_id=1, source_target_pairs={{0,3},{1,2},{2,1},{3,0},{4,7},{5,6},{6,5},{7,4},{8,11},{9,10},{10,... | collective-permute-start | bytes 786440 | tf_op jit(solution)/shard_map/ppermute | solution.py:26
  72.4 33.3 %collective-permute-start.16 = (bf16[256,512]{1,0:T(8,128)(2,1)S(1)}, bf16[256,512]{1,0:T(8,128)(2,1)S(1)}, u32[]{:S(2)}, u32[]{:S(2)}) collective-permute-start(bf16[256,512]{1,0:T(8,128)(2,1)S(1)} %copy-done.1), channel_id=1, source_target_pairs={{0,16},{4,20},{8,24},{12,28},{16,0},{20,4},{24,8},{28,12},{1,17},{... | collective-permute-start | bytes 786440 | tf_op jit(solution)/shard_map/ppermute | solution.py:26
  83.3 22.4 %collective-permute-start.17 = (bf16[256,512]{1,0:T(8,128)(2,1)S(1)}, bf16[256,512]{1,0:T(8,128)(2,1)S(1)}, u32[]{:S(2)}, u32[]{:S(2)}) collective-permute-start(bf16[256,512]{1,0:T(8,128)(2,1)S(1)} %get-tuple-element.46.grad), channel_id=1, source_target_pairs={{0,16},{4,20},{8,24},{12,28},{16,0},{20,4},{24,8},{28,12},{1,17},{... | collective-permute-start | bytes 786440 | tf_op jit(solution)/shard_map/ppermute | solution.py:26
  86.8 8.9 %collective-permute-start.24 = (bf16[128,512]{1,0:T(8,128)(2,1)S(1)}, bf16[128,512]{1,0:T(8,128)(2,1)S(1)}, u32[]{:S(2)}, u32[]{:S(2)}) collective-permute-start(bf16[128,512]{1,0:T(8,128)(2,1)S(1)} %shard_map.119.refs_0_), channel_id=1, source_target_pairs={{0,8},{4,12},{8,0},{12,4},{16,24},{20,28},{24,16},{28,20},{1,9},{5... | collective-permute-start | bytes 393224 | tf_op jit(solution)/shard_map/ppermute | solution.py:26
  86.9 21.3 %collective-permute-start.25 = (bf16[128,512]{1,0:T(8,128)(2,1)S(1)}, bf16[128,512]{1,0:T(8,128)(2,1)S(1)}, u32[]{:S(2)}, u32[]{:S(2)}) collective-permute-start(bf16[128,512]{1,0:T(8,128)(2,1)S(1)} %shard_map.119.refs_0_), channel_id=1, source_target_pairs={{0,4},{4,0},{8,12},{12,8},{16,20},{20,16},{24,28},{28,24},{1,5},{5... | collective-permute-start | bytes 393224 | tf_op jit(solution)/shard_map/ppermute | solution.py:26
  95.8 12.5 %collective-permute-start.26 = (bf16[128,512]{1,0:T(8,128)(2,1)S(1)}, bf16[128,512]{1,0:T(8,128)(2,1)S(1)}, u32[]{:S(2)}, u32[]{:S(2)}) collective-permute-start(bf16[128,512]{1,0:T(8,128)(2,1)S(1)} %collective-permute-done.24.refs_1_), channel_id=1, source_target_pairs={{0,4},{4,0},{8,12},{12,8},{16,20},{20,16},{24,28},{28,24},{1,5},{5... | collective-permute-start | bytes 393224 | tf_op jit(solution)/shard_map/ppermute | solution.py:26

commit v2 on v1

--- a/solution.py
+++ b/solution.py
@@ -222,7 +222,7 @@
             put_columns(stats, rows, head, (top, scale, delta))
         term_out[:, part] = dot(jnp.concatenate(rounded, 0), grad[:, part], TN)
 
-    lax.fori_loop(0, heads, one_head, None, unroll=2)
+    lax.fori_loop(0, heads, one_head, None, unroll=4)
 
 
 def glob_kernel(parts, query, grad, near_stats, weights_in, value_term, *refs):
@@ -255,7 +255,7 @@
         put_columns(stats, every, head, notes, step=heads, width=1)
         put_columns(delta_out, every, head, (delta,))
 
-    lax.fori_loop(0, heads, one_head, None, unroll=2)
+    lax.fori_loop(0, heads, one_head, None, unroll=4)
     groups, lines = note_lines(query.shape[0], query.shape[1])
     for start in range(0, query.shape[0], BLOCK):
         turned = stats[pl.ds(start, BLOCK), :].T
@@ -289,7 +289,7 @@
             query_sum = dot(score_grad, keys) + dot(scores_in[rows, glob], glob_key[:, part])
             query_out[rows, part] = (query_sum * FACTOR).astype(BF16)
 
-    lax.fori_loop(0, heads, one_head, None, unroll=2)
+    lax.fori_loop(0, heads, one_head, None, unroll=4)
 
 
 def key_kernel(s, count, cols_ref, key, value, *refs):
@@ -330,7 +330,7 @@
                 key_out[place, part] += key_term
                 value_out[place, part] += value_term
 
-    lax.fori_loop(0, heads, one_head, None)
+    lax.fori_loop(0, heads, one_head, None, unroll=4)
 
 
 def key_side(source, cols, key, value, pair, message, so_far=()):

time: 110 us -> 108 us (0.982)
  Pallas kernels: 23.2 us -> 20.5 us
  waiting for transfers between devices: 50.2 us -> 51.4 us
    pallas_call x19, Pallas kernels: 23.2 us -> 20.5 us  [call(): pl.pallas_call(kernel, in_specs=in_specs, out_specs=outs, out_shape=out_s...]
    ppermute x27, waiting for transfers between devices: 50.2 us -> 51.4 us  [swap(): lax.ppermute(shard, axis, [(i, i ^ mask) for i in range(lax.axis_size(axi...]
  transfers between devices with their start and end apart: 27 -> 27, of which waited for: 11 -> 11; matrix products, arithmetic and copies ran while one was open for 0% -> 0% of each run, Pallas kernels for 20% -> 18%
where the time goes in v2:
time: 108 us
  waiting for transfers between devices  51.4 us (48%)
  starting transfers between devices  32.6 us (30%)
  Pallas kernels  20.5 us (19%)
  local copies, waits for them, and re-layouts  2.6 us (2%)
    ppermute x27, waiting for transfers between devices, swap(): lax.ppermute(shard, axis, [(i, i ^ mask) for i in range(lax.axis_size(axi...  51.4 us
    ppermute x27, starting transfers between devices, swap(): lax.ppermute(shard, axis, [(i, i ^ mask) for i in range(lax.axis_size(axi...  32.6 us
    pallas_call x19, Pallas kernels, call(): pl.pallas_call(kernel, in_specs=in_specs, out_specs=outs, out_shape=out_s...  20.5 us
    unnamed x14, local copies, waits for them, and re-layouts  2.6 us
  transfers between devices with their start and end apart: 27, of which 11 were waited for; matrix products, arithmetic and copies ran while one was open for 0% of the time, Pallas kernels for 18%

profile of v2, /device:TPU:0, one launch (start us, length us, event | category | flops | bytes accessed | tf_op | source)
XLA Modules:
  0.0 107.9 jit_solution(647555259269843412)
XLA Ops:
  0.6 3.1 %collective-permute-start.3 = (bf16[256,512]{1,0:T(8,128)(2,1)}, bf16[256,512]{1,0:T(8,128)(2,1)S(1)}, u32[]{:S(2)}, u32[]{:S(2)}) collective-permute-start(bf16[256,512]{1,0:T(8,128)(2,1)} %key.1), channel_id=1, source_target_pairs={{0,4},{4,0},{8,12},{12,8},{16,20},{20,16},{24,28},{28,24},{1,5},{5... | collective-permute-start | bytes 786440 | tf_op jit(solution)/shard_map/ppermute | solution.py:26
  3.7 1.6 %collective-permute-start.4 = (bf16[256,512]{1,0:T(8,128)(2,1)}, bf16[256,512]{1,0:T(8,128)(2,1)S(1)}, u32[]{:S(2)}, u32[]{:S(2)}) collective-permute-start(bf16[256,512]{1,0:T(8,128)(2,1)} %key.1), channel_id=1, source_target_pairs={{0,8},{4,12},{8,0},{12,4},{16,24},{20,28},{24,16},{28,20},{1,9},{5... | collective-permute-start | bytes 786440 | tf_op jit(solution)/shard_map/ppermute | solution.py:26
  5.3 2.6 %collective-permute-start.5 = (bf16[256,512]{1,0:T(8,128)(2,1)}, bf16[256,512]{1,0:T(8,128)(2,1)S(1)}, u32[]{:S(2)}, u32[]{:S(2)}) collective-permute-start(bf16[256,512]{1,0:T(8,128)(2,1)} %key.1), channel_id=1, source_target_pairs={{0,16},{4,20},{8,24},{12,28},{16,0},{20,4},{24,8},{28,12},{1,17},{... | collective-permute-start | bytes 786440 | tf_op jit(solution)/shard_map/ppermute | solution.py:26
  7.9 0.5 collective-permute-start.6
  8.4 0.4 collective-permute-start.7
  8.8 1.9 %collective-permute-done.3.refs_5_.refs_2_.refs_4_ = bf16[256,512]{1,0:T(8,128)(2,1)S(1)} collective-permute-done((bf16[256,512]{1,0:T(8,128)(2,1)}, bf16[256,512]{1,0:T(8,128)(2,1)S(1)}, u32[]{:S(2)}, u32[]{:S(2)}) %collective-permute-start.3) | collective-permute-done | bytes 262176 | tf_op jit(solution)/shard_map/ppermute | solution.py:26
  10.8 3.4 %collective-permute-start.8 = (bf16[256,512]{1,0:T(8,128)(2,1)}, bf16[256,512]{1,0:T(8,128)(2,1)S(1)}, u32[]{:S(2)}, u32[]{:S(2)}) collective-permute-start(bf16[256,512]{1,0:T(8,128)(2,1)} %value.1), channel_id=1, source_target_pairs={{0,16},{4,20},{8,24},{12,28},{16,0},{20,4},{24,8},{28,12},{1,17},{... | collective-permute-start | bytes 786440 | tf_op jit(solution)/shard_map/ppermute | solution.py:26
  14.2 0.9 copy-done.2
  15.1 0.9 copy-done.3
  16.1 0.7 copy-done.6
  17.0 2.1 %collective-permute-done.4.refs_6_.refs_3_.refs_5_ = bf16[256,512]{1,0:T(8,128)(2,1)S(1)} collective-permute-done((bf16[256,512]{1,0:T(8,128)(2,1)}, bf16[256,512]{1,0:T(8,128)(2,1)S(1)}, u32[]{:S(2)}, u32[]{:S(2)}) %collective-permute-start.4) | collective-permute-done | bytes 262176 | tf_op jit(solution)/shard_map/ppermute | solution.py:26
  19.1 1.7 %collective-permute-done.5.refs_7_.refs_4_.refs_6_ = bf16[256,512]{1,0:T(8,128)(2,1)S(1)} collective-permute-done((bf16[256,512]{1,0:T(8,128)(2,1)}, bf16[256,512]{1,0:T(8,128)(2,1)S(1)}, u32[]{:S(2)}, u32[]{:S(2)}) %collective-permute-start.5) | collective-permute-done | bytes 262176 | tf_op jit(solution)/shard_map/ppermute | solution.py:26
  20.7 0.4 shard_map.104.have
  21.3 7.1 %collective-permute-done.7.refs_6_.refs_8_ = bf16[256,512]{1,0:T(8,128)(2,1)S(1)} collective-permute-done((bf16[256,512]{1,0:T(8,128)(2,1)}, bf16[256,512]{1,0:T(8,128)(2,1)S(1)}, u32[]{:S(2)}, u32[]{:S(2)}) %collective-permute-start.7) | collective-permute-done | bytes 262176 | tf_op jit(solution)/shard_map/ppermute | solution.py:26
  28.4 2.4 %collective-permute-done.8.refs_7_.refs_9_ = bf16[256,512]{1,0:T(8,128)(2,1)S(1)} collective-permute-done((bf16[256,512]{1,0:T(8,128)(2,1)}, bf16[256,512]{1,0:T(8,128)(2,1)S(1)}, u32[]{:S(2)}, u32[]{:S(2)}) %collective-permute-start.8) | collective-permute-done | bytes 262176 | tf_op jit(solution)/shard_map/ppermute | solution.py:26
  30.8 0.4 shard_map.107.have
  31.3 0.6 collective-permute-start.11
  31.8 1.5 %collective-permute-start.1 = (bf16[256,512]{1,0:T(8,128)(2,1)S(1)}, bf16[256,512]{1,0:T(8,128)(2,1)S(1)}, u32[]{:S(2)}, u32[]{:S(2)}) collective-permute-start(bf16[256,512]{1,0:T(8,128)(2,1)S(1)} %copy-done.4), channel_id=1, source_target_pairs={{0,2},{1,3},{2,0},{3,1},{4,6},{5,7},{6,4},{7,5},{8,10},{9,11},{10,... | collective-permute-start | bytes 786440 | tf_op jit(solution)/shard_map/ppermute | solution.py:26
  33.8 0.5 collective-permute-start.10
  34.3 3.4 %collective-permute-done.11.got = bf16[256,512]{1,0:T(8,128)(2,1)S(1)} collective-permute-done((bf16[256,512]{1,0:T(8,128)(2,1)S(1)}, bf16[256,512]{1,0:T(8,128)(2,1)S(1)}, u32[]{:S(2)}, u32[]{:S(2)}) %collective-permute-start.11) | collective-permute-done | bytes 262176 | tf_op jit(solution)/shard_map/ppermute | solution.py:26
  37.8 1.0 collective-permute-start.12
  38.8 2.2 %collective-permute-done.1.refs_2_ = bf16[256,512]{1,0:T(8,128)(2,1)S(1)} collective-permute-done((bf16[256,512]{1,0:T(8,128)(2,1)S(1)}, bf16[256,512]{1,0:T(8,128)(2,1)S(1)}, u32[]{:S(2)}, u32[]{:S(2)}) %collective-permute-start.1) | collective-permute-done | bytes 262176 | tf_op jit(solution)/shard_map/ppermute | solution.py:26
  41.0 4.7 %collective-permute-done.2.refs_3_ = bf16[256,512]{1,0:T(8,128)(2,1)S(1)} collective-permute-done((bf16[256,512]{1,0:T(8,128)(2,1)S(1)}, bf16[256,512]{1,0:T(8,128)(2,1)S(1)}, u32[]{:S(2)}, u32[]{:S(2)}) %collective-permute-start.2) | collective-permute-done | bytes 262176 | tf_op jit(solution)/shard_map/ppermute | solution.py:26
  45.7 0.7 shard_map.102
  46.5 1.6 %collective-permute-start.23 = (bf16[512,512]{1,0:T(8,128)(2,1)S(1)}, bf16[512,512]{1,0:T(8,128)(2,1)S(1)}, u32[]{:S(2)}, u32[]{:S(2)}) collective-permute-start(bf16[512,512]{1,0:T(8,128)(2,1)S(1)} %get-tuple-element.76.refs_0_), channel_id=1, source_target_pairs={{0,4},{4,0},{8,12},{12,8},{16,20},{20,16},{24,28},{28,24},{1,5},{5... | collective-permute-start | bytes 1572872 | tf_op jit(solution)/shard_map/ppermute | solution.py:26
  48.1 3.3 %shard_map.106 = (f32[256,2048]{1,0:T(8,128)S(1)}, f32[256,2048]{1,0:T(8,128)S(1)}, f32[256,1024]{1,0:T(8,128)S(1)}, f32[256,512]{1,0:T(8,128)S(1)}, bf16[256,51...) custom-call(s32[3,16]{1,0:T(4,128)S(1)} %bitcast.2, bf16[256,512]{1,0:T(8,128)(2,1)S(1)} %copy-done.1, ...), custom_call_target="tpu_custom_call" | custom-call | tf_op jit(solution)/shard_map/pallas_call | solution.py:34
  51.4 1.3 %shard_map.109 = (f32[128,512]{1,0:T(8,128)S(1)}, f32[128,512]{1,0:T(8,128)S(1)}, bf16[128,512]{1,0:T(8,128)(2,1)S(1)}, bf16[144,512]{1,0:T(8,128)(2,1)S(1)}, f3...) custom-call(bf16[256,512]{1,0:T(8,128)(2,1)S(1)} %copy-done.1, ...), custom_call_target="tpu_custom_call" | custom-call | tf_op jit(solution)/shard_map/pallas_call | solution.py:34
  52.7 0.6 collective-permute-start.19
  53.2 1.5 %collective-permute-start.18 = (bf16[144,512]{1,0:T(8,128)(2,1)S(1)}, bf16[144,512]{1,0:T(8,128)(2,1)S(1)}, u32[]{:S(2)}, u32[]{:S(2)}) collective-permute-start(bf16[144,512]{1,0:T(8,128)(2,1)S(1)} %get-tuple-element.72.refs_2_.refs_3_.refs_1_), channel_id=1, source_target_pairs={{0,4},{4,0},{8,12},{12,8},{16,20},{20,16},{24,28},{28,24},{1,5},{5... | collective-permute-start | bytes 442376 | tf_op jit(solution)/shard_map/ppermute | solution.py:26
  54.7 9.4 %collective-permute-done.19.refs_1_ = bf16[128,512]{1,0:T(8,128)(2,1)S(1)} collective-permute-done((bf16[128,512]{1,0:T(8,128)(2,1)S(1)}, bf16[128,512]{1,0:T(8,128)(2,1)S(1)}, u32[]{:S(2)}, u32[]{:S(2)}) %collective-permute-start.19) | collective-permute-done | bytes 131104 | tf_op jit(solution)/shard_map/ppermute | solution.py:26
  64.2 0.5 collective-permute-start.20
  64.7 1.6 %collective-permute-start.22 = (bf16[512,512]{1,0:T(8,128)(2,1)S(1)}, bf16[512,512]{1,0:T(8,128)(2,1)S(1)}, u32[]{:S(2)}, u32[]{:S(2)}) collective-permute-start(bf16[512,512]{1,0:T(8,128)(2,1)S(1)} %get-tuple-element.76.refs_0_), channel_id=1, source_target_pairs={{0,8},{4,12},{8,0},{12,4},{16,24},{20,28},{24,16},{28,20},{1,9},{5... | collective-permute-start | bytes 1572872 | tf_op jit(solution)/shard_map/ppermute | solution.py:26
  66.3 2.4 %shard_map.110 = (bf16[256,512]{1,0:T(8,128)(2,1)S(1)}, bf16[256,512]{1,0:T(8,128)(2,1)}) custom-call(s32[3,16]{1,0:T(4,128)S(1)} %bitcast.3, f32[256,2048]{1,0:T(8,128)S(1)} %get-tuple-element.55.weights_in, f32[256,2048]{1,0:T(8,128)S(1)} %get-tuple-element.56.probs, f32[256,128]{1,0:T(8,128)S(1)} %get-tuple-element.60.deltas, ...), custom_call_target="tpu_custom_call" | custom-call | tf_op jit(solution)/shard_map/pallas_call | solution.py:34
  68.7 0.7 shard_map.111
  69.5 1.6 %collective-permute-start.14 = (bf16[256,512]{1,0:T(8,128)(2,1)S(1)}, bf16[256,512]{1,0:T(8,128)(2,1)S(1)}, u32[]{:S(2)}, u32[]{:S(2)}) collective-permute-start(bf16[256,512]{1,0:T(8,128)(2,1)S(1)} %get-tuple-element.67), channel_id=1, source_target_pairs={{0,2},{1,3},{2,0},{3,1},{4,6},{5,7},{6,4},{7,5},{8,10},{9,11},{10,... | collective-permute-start | bytes 786440 | tf_op jit(solution)/shard_map/ppermute | solution.py:26
  71.1 1.1 %collective-permute-start.21 = (bf16[144,512]{1,0:T(8,128)(2,1)S(1)}, bf16[144,512]{1,0:T(8,128)(2,1)S(1)}, u32[]{:S(2)}, u32[]{:S(2)}) collective-permute-start(bf16[144,512]{1,0:T(8,128)(2,1)S(1)} %get-tuple-element.75), channel_id=1, source_target_pairs={{0,16},{4,20},{8,24},{12,28},{16,0},{20,4},{24,8},{28,12},{1,17},{... | collective-permute-start | bytes 442376 | tf_op jit(solution)/shard_map/ppermute | solution.py:26
  72.3 1.9 %collective-permute-start.16 = (bf16[256,512]{1,0:T(8,128)(2,1)S(1)}, bf16[256,512]{1,0:T(8,128)(2,1)S(1)}, u32[]{:S(2)}, u32[]{:S(2)}) collective-permute-start(bf16[256,512]{1,0:T(8,128)(2,1)S(1)} %copy-done.1), channel_id=1, source_target_pairs={{0,16},{4,20},{8,24},{12,28},{16,0},{20,4},{24,8},{28,12},{1,17},{... | collective-permute-start | bytes 786440 | tf_op jit(solution)/shard_map/ppermute | solution.py:26
  74.2 9.2 %collective-permute-done.21.refs_2_.refs_1_ = bf16[144,512]{1,0:T(8,128)(2,1)S(1)} collective-permute-done((bf16[144,512]{1,0:T(8,128)(2,1)S(1)}, bf16[144,512]{1,0:T(8,128)(2,1)S(1)}, u32[]{:S(2)}, u32[]{:S(2)}) %collective-permute-start.21) | collective-permute-done | bytes 147488 | tf_op jit(solution)/shard_map/ppermute | solution.py:26
  83.3 3.4 %collective-permute-start.17 = (bf16[256,512]{1,0:T(8,128)(2,1)S(1)}, bf16[256,512]{1,0:T(8,128)(2,1)S(1)}, u32[]{:S(2)}, u32[]{:S(2)}) collective-permute-start(bf16[256,512]{1,0:T(8,128)(2,1)S(1)} %get-tuple-element.46.grad), channel_id=1, source_target_pairs={{0,16},{4,20},{8,24},{12,28},{16,0},{20,4},{24,8},{28,12},{1,17},{... | collective-permute-start | bytes 786440 | tf_op jit(solution)/shard_map/ppermute | solution.py:26
  86.9 1.6 %collective-permute-start.25 = (bf16[128,512]{1,0:T(8,128)(2,1)S(1)}, bf16[128,512]{1,0:T(8,128)(2,1)S(1)}, u32[]{:S(2)}, u32[]{:S(2)}) collective-permute-start(bf16[128,512]{1,0:T(8,128)(2,1)S(1)} %shard_map.119.refs_0_), channel_id=1, source_target_pairs={{0,4},{4,0},{8,12},{12,8},{16,20},{20,16},{24,28},{28,24},{1,5},{5... | collective-permute-start | bytes 393224 | tf_op jit(solution)/shard_map/ppermute | solution.py:26
  88.5 7.3 %collective-permute-done.24.refs_1_ = bf16[128,512]{1,0:T(8,128)(2,1)S(1)} collective-permute-done((bf16[128,512]{1,0:T(8,128)(2,1)S(1)}, bf16[128,512]{1,0:T(8,128)(2,1)S(1)}, u32[]{:S(2)}, u32[]{:S(2)}) %collective-permute-start.24) | collective-permute-done | bytes 131104 | tf_op jit(solution)/shard_map/ppermute | solution.py:26
  95.8 1.5 %collective-permute-start.26 = (bf16[128,512]{1,0:T(8,128)(2,1)S(1)}, bf16[128,512]{1,0:T(8,128)(2,1)S(1)}, u32[]{:S(2)}, u32[]{:S(2)}) collective-permute-start(bf16[128,512]{1,0:T(8,128)(2,1)S(1)} %collective-permute-done.24.refs_1_), channel_id=1, source_target_pairs={{0,4},{4,0},{8,12},{12,8},{16,20},{20,16},{24,28},{28,24},{1,5},{5... | collective-permute-start | bytes 393224 | tf_op jit(solution)/shard_map/ppermute | solution.py:26
  97.3 2.1 %shard_map.115 = (f32[256,512]{1,0:T(8,128)S(1)}, f32[256,512]{1,0:T(8,128)S(1)}) custom-call(s32[3,16]{1,0:T(4,128)S(1)} %bitcast.4, bf16[256,512]{1,0:T(8,128)(2,1)S(1)} %get-tuple-element.47.refs_4_.refs_0_.refs_2_.key, bf16[256,512]{1,0:T(8,128)(2,1)S(1)} %get-tuple-element.48.refs_1_.refs_4_.refs_3_.value, ...), custom_call_target="tpu_custom_call" | custom-call | tf_op jit(solution)/shard_map/pallas_call | solution.py:34
  99.4 2.2 %shard_map.116 = (f32[256,512]{1,0:T(8,128)S(1)}, f32[256,512]{1,0:T(8,128)S(1)}) custom-call(s32[3,16]{1,0:T(4,128)S(1)} %bitcast.5, bf16[256,512]{1,0:T(8,128)(2,1)S(1)} %get-tuple-element.47.refs_4_.refs_0_.refs_2_.key, bf16[256,512]{1,0:T(8,128)(2,1)S(1)} %get-tuple-element.48.refs_1_.refs_4_.refs_3_.value, ...), custom_call_target="tpu_custom_call" | custom-call | tf_op jit(solution)/shard_map/pallas_call | solution.py:34
  101.5 0.8 shard_map.112
  102.4 2.1 %shard_map.117 = (f32[256,512]{1,0:T(8,128)S(1)}, f32[256,512]{1,0:T(8,128)S(1)}) custom-call(s32[3,16]{1,0:T(4,128)S(1)} %bitcast.6, bf16[256,512]{1,0:T(8,128)(2,1)S(1)} %get-tuple-element.47.refs_4_.refs_0_.refs_2_.key, bf16[256,512]{1,0:T(8,128)(2,1)S(1)} %get-tuple-element.48.refs_1_.refs_4_.refs_3_.value, ...), custom_call_target="tpu_custom_call" | custom-call | tf_op jit(solution)/shard_map/pallas_call | solution.py:34
  104.5 2.2 %shard_map.118 = (f32[256,512]{1,0:T(8,128)S(1)}, f32[256,512]{1,0:T(8,128)S(1)}) custom-call(s32[3,16]{1,0:T(4,128)S(1)} %bitcast.7, bf16[256,512]{1,0:T(8,128)(2,1)S(1)} %get-tuple-element.47.refs_4_.refs_0_.refs_2_.key, bf16[256,512]{1,0:T(8,128)(2,1)S(1)} %get-tuple-element.48.refs_1_.refs_4_.refs_3_.value, ...), custom_call_target="tpu_custom_call" | custom-call | tf_op jit(solution)/shard_map/pallas_call | solution.py:34
  106.7 1.2 %shard_map.120 = (bf16[256,512]{1,0:T(8,128)(2,1)}, bf16[256,512]{1,0:T(8,128)(2,1)}) custom-call(bf16[256,256]{1,0:T(8,128)(2,1)S(1)} %get-tuple-element.70.scatter, f32[256,512]{1,0:T(8,128)S(1)} %get-tuple-element.83.key, f32[256,512]{1,0:T(8,128)S(1)} %get-tuple-element.84.value, bf16[128,512]{1,0:T(8,128)(2,1)S(1)} %shard_map.119.refs_0_, ...), custom_call_target="tpu_custom_call" | custom-call | tf_op jit(solution)/shard_map/pallas_call | solution.py:34
  (39 shorter events, 1.2 us)
Async XLA Ops:
  0.6 10.1 %collective-permute-start.3 = (bf16[256,512]{1,0:T(8,128)(2,1)}, bf16[256,512]{1,0:T(8,128)(2,1)S(1)}, u32[]{:S(2)}, u32[]{:S(2)}) collective-permute-start(bf16[256,512]{1,0:T(8,128)(2,1)} %key.1), channel_id=1, source_target_pairs={{0,4},{4,0},{8,12},{12,8},{16,20},{20,16},{24,28},{28,24},{1,5},{5... | collective-permute-start | bytes 786440 | tf_op jit(solution)/shard_map/ppermute | solution.py:26
  3.7 15.4 %collective-permute-start.4 = (bf16[256,512]{1,0:T(8,128)(2,1)}, bf16[256,512]{1,0:T(8,128)(2,1)S(1)}, u32[]{:S(2)}, u32[]{:S(2)}) collective-permute-start(bf16[256,512]{1,0:T(8,128)(2,1)} %key.1), channel_id=1, source_target_pairs={{0,8},{4,12},{8,0},{12,4},{16,24},{20,28},{24,16},{28,20},{1,9},{5... | collective-permute-start | bytes 786440 | tf_op jit(solution)/shard_map/ppermute | solution.py:26
  5.3 15.5 %collective-permute-start.5 = (bf16[256,512]{1,0:T(8,128)(2,1)}, bf16[256,512]{1,0:T(8,128)(2,1)S(1)}, u32[]{:S(2)}, u32[]{:S(2)}) collective-permute-start(bf16[256,512]{1,0:T(8,128)(2,1)} %key.1), channel_id=1, source_target_pairs={{0,16},{4,20},{8,24},{12,28},{16,0},{20,4},{24,8},{28,12},{1,17},{... | collective-permute-start | bytes 786440 | tf_op jit(solution)/shard_map/ppermute | solution.py:26
  7.9 13.4 %collective-permute-start.6 = (bf16[256,512]{1,0:T(8,128)(2,1)}, bf16[256,512]{1,0:T(8,128)(2,1)S(1)}, u32[]{:S(2)}, u32[]{:S(2)}) collective-permute-start(bf16[256,512]{1,0:T(8,128)(2,1)} %value.1), channel_id=1, source_target_pairs={{0,4},{4,0},{8,12},{12,8},{16,20},{20,16},{24,28},{28,24},{1,5},{5... | collective-permute-start | bytes 786440 | tf_op jit(solution)/shard_map/ppermute | solution.py:26
  8.4 20.0 %collective-permute-start.7 = (bf16[256,512]{1,0:T(8,128)(2,1)}, bf16[256,512]{1,0:T(8,128)(2,1)S(1)}, u32[]{:S(2)}, u32[]{:S(2)}) collective-permute-start(bf16[256,512]{1,0:T(8,128)(2,1)} %value.1), channel_id=1, source_target_pairs={{0,8},{4,12},{8,0},{12,4},{16,24},{20,28},{24,16},{28,20},{1,9},{5... | collective-permute-start | bytes 786440 | tf_op jit(solution)/shard_map/ppermute | solution.py:26
  10.8 20.1 %collective-permute-start.8 = (bf16[256,512]{1,0:T(8,128)(2,1)}, bf16[256,512]{1,0:T(8,128)(2,1)S(1)}, u32[]{:S(2)}, u32[]{:S(2)}) collective-permute-start(bf16[256,512]{1,0:T(8,128)(2,1)} %value.1), channel_id=1, source_target_pairs={{0,16},{4,20},{8,24},{12,28},{16,0},{20,4},{24,8},{28,12},{1,17},{... | collective-permute-start | bytes 786440 | tf_op jit(solution)/shard_map/ppermute | solution.py:26
  14.1 0.9 copy-start.2
  15.1 0.9 copy-start.3
  16.1 0.7 copy-start.6
  16.7 15.1 %copy-start.4 = (bf16[256,512]{1,0:T(8,128)(2,1)S(1)}, bf16[256,512]{1,0:T(8,128)(2,1)}, u32[]{:S(2)}) copy-start(bf16[256,512]{1,0:T(8,128)(2,1)} %refs_0_.1) | copy-start | bytes 786436
  21.2 24.6 %copy-start = (bf16[512,2048]{1,0:T(8,128)(2,1)S(1)}, bf16[512,2048]{1,0:T(8,128)(2,1)}, u32[]{:S(2)}) copy-start(bf16[512,2048]{1,0:T(8,128)(2,1)} %weight_ref.3) | copy-start | bytes 6291460
  21.2 24.5 %copy-start.1 = (bf16[256,512]{1,0:T(8,128)(2,1)S(1)}, bf16[256,512]{1,0:T(8,128)(2,1)}, u32[]{:S(2)}) copy-start(bf16[256,512]{1,0:T(8,128)(2,1)} %query.5) | copy-start | bytes 786436
  21.2 12.5 %collective-permute-start.9 = (bf16[256,512]{1,0:T(8,128)(2,1)S(1)}, bf16[256,512]{1,0:T(8,128)(2,1)S(1)}, u32[]{:S(2)}, u32[]{:S(2)}) collective-permute-start(bf16[256,512]{1,0:T(8,128)(2,1)S(1)} %shard_map.104.have), channel_id=1, source_target_pairs={{0,4},{4,0},{8,12},{12,8},{16,20},{20,16},{24,28},{28,24},{1,5},{5... | collective-permute-start | bytes 786440 | tf_op jit(solution)/shard_map/ppermute | solution.py:26
  31.3 6.4 %collective-permute-start.11 = (bf16[256,512]{1,0:T(8,128)(2,1)S(1)}, bf16[256,512]{1,0:T(8,128)(2,1)S(1)}, u32[]{:S(2)}, u32[]{:S(2)}) collective-permute-start(bf16[256,512]{1,0:T(8,128)(2,1)S(1)} %shard_map.107.have), channel_id=1, source_target_pairs={{0,4},{4,0},{8,12},{12,8},{16,20},{20,16},{24,28},{28,24},{1,5},{5... | collective-permute-start | bytes 786440 | tf_op jit(solution)/shard_map/ppermute | solution.py:26
  31.8 6.9 %collective-permute-start = (bf16[256,512]{1,0:T(8,128)(2,1)S(1)}, bf16[256,512]{1,0:T(8,128)(2,1)S(1)}, u32[]{:S(2)}, u32[]{:S(2)}) collective-permute-start(bf16[256,512]{1,0:T(8,128)(2,1)S(1)} %copy-done.4), channel_id=1, source_target_pairs={{0,1},{1,0},{2,3},{3,2},{4,5},{5,4},{6,7},{7,6},{8,9},{9,8},{10,11... | collective-permute-start | bytes 786440 | tf_op jit(solution)/shard_map/ppermute | solution.py:26
  31.8 9.2 %collective-permute-start.1 = (bf16[256,512]{1,0:T(8,128)(2,1)S(1)}, bf16[256,512]{1,0:T(8,128)(2,1)S(1)}, u32[]{:S(2)}, u32[]{:S(2)}) collective-permute-start(bf16[256,512]{1,0:T(8,128)(2,1)S(1)} %copy-done.4), channel_id=1, source_target_pairs={{0,2},{1,3},{2,0},{3,1},{4,6},{5,7},{6,4},{7,5},{8,10},{9,11},{10,... | collective-permute-start | bytes 786440 | tf_op jit(solution)/shard_map/ppermute | solution.py:26
  33.3 12.4 %collective-permute-start.2 = (bf16[256,512]{1,0:T(8,128)(2,1)S(1)}, bf16[256,512]{1,0:T(8,128)(2,1)S(1)}, u32[]{:S(2)}, u32[]{:S(2)}) collective-permute-start(bf16[256,512]{1,0:T(8,128)(2,1)S(1)} %copy-done.4), channel_id=1, source_target_pairs={{0,3},{1,2},{2,1},{3,0},{4,7},{5,6},{6,5},{7,4},{8,11},{9,10},{10,... | collective-permute-start | bytes 786440 | tf_op jit(solution)/shard_map/ppermute | solution.py:26
  33.8 14.3 %copy-start.5 = (s32[16,3]{0,1:T(4,128)S(1)}, s32[16,3]{0,1:T(4,128)}, u32[]{:S(2)}) copy-start(s32[16,3]{0,1:T(4,128)} %param.12) | copy-start | bytes 580
  33.8 14.2 %collective-permute-start.10 = (bf16[256,512]{1,0:T(8,128)(2,1)S(1)}, bf16[256,512]{1,0:T(8,128)(2,1)S(1)}, u32[]{:S(2)}, u32[]{:S(2)}) collective-permute-start(bf16[256,512]{1,0:T(8,128)(2,1)S(1)} %shard_map.105.refs_8_), channel_id=1, source_target_pairs={{0,8},{4,12},{8,0},{12,4},{16,24},{20,28},{24,16},{28,20},{1,9},{5... | collective-permute-start | bytes 786440 | tf_op jit(solution)/shard_map/ppermute | solution.py:26
  37.8 13.5 %collective-permute-start.12 = (bf16[256,512]{1,0:T(8,128)(2,1)S(1)}, bf16[256,512]{1,0:T(8,128)(2,1)S(1)}, u32[]{:S(2)}, u32[]{:S(2)}) collective-permute-start(bf16[256,512]{1,0:T(8,128)(2,1)S(1)} %shard_map.108.refs_0_), channel_id=1, source_target_pairs={{0,8},{4,12},{8,0},{12,4},{16,24},{20,28},{24,16},{28,20},{1,9},{5... | collective-permute-start | bytes 786440 | tf_op jit(solution)/shard_map/ppermute | solution.py:26
  46.5 25.8 %collective-permute-start.23 = (bf16[512,512]{1,0:T(8,128)(2,1)S(1)}, bf16[512,512]{1,0:T(8,128)(2,1)S(1)}, u32[]{:S(2)}, u32[]{:S(2)}) collective-permute-start(bf16[512,512]{1,0:T(8,128)(2,1)S(1)} %get-tuple-element.76.refs_0_), channel_id=1, source_target_pairs={{0,4},{4,0},{8,12},{12,8},{16,20},{20,16},{24,28},{28,24},{1,5},{5... | collective-permute-start | bytes 1572872 | tf_op jit(solution)/shard_map/ppermute | solution.py:26
  52.7 11.5 %collective-permute-start.19 = (bf16[128,512]{1,0:T(8,128)(2,1)S(1)}, bf16[128,512]{1,0:T(8,128)(2,1)S(1)}, u32[]{:S(2)}, u32[]{:S(2)}) collective-permute-start(bf16[128,512]{1,0:T(8,128)(2,1)S(1)} %get-tuple-element.74), channel_id=1, source_target_pairs={{0,4},{4,0},{8,12},{12,8},{16,20},{20,16},{24,28},{28,24},{1,5},{5... | collective-permute-start | bytes 393224 | tf_op jit(solution)/shard_map/ppermute | solution.py:26
  53.2 16.3 %collective-permute-start.18 = (bf16[144,512]{1,0:T(8,128)(2,1)S(1)}, bf16[144,512]{1,0:T(8,128)(2,1)S(1)}, u32[]{:S(2)}, u32[]{:S(2)}) collective-permute-start(bf16[144,512]{1,0:T(8,128)(2,1)S(1)} %get-tuple-element.72.refs_2_.refs_3_.refs_1_), channel_id=1, source_target_pairs={{0,4},{4,0},{8,12},{12,8},{16,20},{20,16},{24,28},{28,24},{1,5},{5... | collective-permute-start | bytes 442376 | tf_op jit(solution)/shard_map/ppermute | solution.py:26
  64.2 6.9 %collective-permute-start.20 = (bf16[144,512]{1,0:T(8,128)(2,1)S(1)}, bf16[144,512]{1,0:T(8,128)(2,1)S(1)}, u32[]{:S(2)}, u32[]{:S(2)}) collective-permute-start(bf16[144,512]{1,0:T(8,128)(2,1)S(1)} %shard_map.113), channel_id=1, source_target_pairs={{0,8},{4,12},{8,0},{12,4},{16,24},{20,28},{24,16},{28,20},{1,9},{5... | collective-permute-start | bytes 442376 | tf_op jit(solution)/shard_map/ppermute | solution.py:26
  64.7 37.7 %collective-permute-start.22 = (bf16[512,512]{1,0:T(8,128)(2,1)S(1)}, bf16[512,512]{1,0:T(8,128)(2,1)S(1)}, u32[]{:S(2)}, u32[]{:S(2)}) collective-permute-start(bf16[512,512]{1,0:T(8,128)(2,1)S(1)} %get-tuple-element.76.refs_0_), channel_id=1, source_target_pairs={{0,8},{4,12},{8,0},{12,4},{16,24},{20,28},{24,16},{28,20},{1,9},{5... | collective-permute-start | bytes 1572872 | tf_op jit(solution)/shard_map/ppermute | solution.py:26
  69.4 2.9 %collective-permute-start.13 = (bf16[256,512]{1,0:T(8,128)(2,1)S(1)}, bf16[256,512]{1,0:T(8,128)(2,1)S(1)}, u32[]{:S(2)}, u32[]{:S(2)}) collective-permute-start(bf16[256,512]{1,0:T(8,128)(2,1)S(1)} %get-tuple-element.66), channel_id=1, source_target_pairs={{0,1},{1,0},{2,3},{3,2},{4,5},{5,4},{6,7},{7,6},{8,9},{9,8},{10,11... | collective-permute-start | bytes 786440 | tf_op jit(solution)/shard_map/ppermute | solution.py:26
  69.5 17.3 %collective-permute-start.14 = (bf16[256,512]{1,0:T(8,128)(2,1)S(1)}, bf16[256,512]{1,0:T(8,128)(2,1)S(1)}, u32[]{:S(2)}, u32[]{:S(2)}) collective-permute-start(bf16[256,512]{1,0:T(8,128)(2,1)S(1)} %get-tuple-element.67), channel_id=1, source_target_pairs={{0,2},{1,3},{2,0},{3,1},{4,6},{5,7},{6,4},{7,5},{8,10},{9,11},{10,... | collective-permute-start | bytes 786440 | tf_op jit(solution)/shard_map/ppermute | solution.py:26
  71.1 12.2 %collective-permute-start.21 = (bf16[144,512]{1,0:T(8,128)(2,1)S(1)}, bf16[144,512]{1,0:T(8,128)(2,1)S(1)}, u32[]{:S(2)}, u32[]{:S(2)}) collective-permute-start(bf16[144,512]{1,0:T(8,128)(2,1)S(1)} %get-tuple-element.75), channel_id=1, source_target_pairs={{0,16},{4,20},{8,24},{12,28},{16,0},{20,4},{24,8},{28,12},{1,17},{... | collective-permute-start | bytes 442376 | tf_op jit(solution)/shard_map/ppermute | solution.py:26
  72.2 14.7 %collective-permute-start.15 = (bf16[256,512]{1,0:T(8,128)(2,1)S(1)}, bf16[256,512]{1,0:T(8,128)(2,1)S(1)}, u32[]{:S(2)}, u32[]{:S(2)}) collective-permute-start(bf16[256,512]{1,0:T(8,128)(2,1)S(1)} %get-tuple-element.68), channel_id=1, source_target_pairs={{0,3},{1,2},{2,1},{3,0},{4,7},{5,6},{6,5},{7,4},{8,11},{9,10},{10,... | collective-permute-start | bytes 786440 | tf_op jit(solution)/shard_map/ppermute | solution.py:26
  72.3 32.3 %collective-permute-start.16 = (bf16[256,512]{1,0:T(8,128)(2,1)S(1)}, bf16[256,512]{1,0:T(8,128)(2,1)S(1)}, u32[]{:S(2)}, u32[]{:S(2)}) collective-permute-start(bf16[256,512]{1,0:T(8,128)(2,1)S(1)} %copy-done.1), channel_id=1, source_target_pairs={{0,16},{4,20},{8,24},{12,28},{16,0},{20,4},{24,8},{28,12},{1,17},{... | collective-permute-start | bytes 786440 | tf_op jit(solution)/shard_map/ppermute | solution.py:26
  83.3 21.2 %collective-permute-start.17 = (bf16[256,512]{1,0:T(8,128)(2,1)S(1)}, bf16[256,512]{1,0:T(8,128)(2,1)S(1)}, u32[]{:S(2)}, u32[]{:S(2)}) collective-permute-start(bf16[256,512]{1,0:T(8,128)(2,1)S(1)} %get-tuple-element.46.grad), channel_id=1, source_target_pairs={{0,16},{4,20},{8,24},{12,28},{16,0},{20,4},{24,8},{28,12},{1,17},{... | collective-permute-start | bytes 786440 | tf_op jit(solution)/shard_map/ppermute | solution.py:26
  86.8 8.9 %collective-permute-start.24 = (bf16[128,512]{1,0:T(8,128)(2,1)S(1)}, bf16[128,512]{1,0:T(8,128)(2,1)S(1)}, u32[]{:S(2)}, u32[]{:S(2)}) collective-permute-start(bf16[128,512]{1,0:T(8,128)(2,1)S(1)} %shard_map.119.refs_0_), channel_id=1, source_target_pairs={{0,8},{4,12},{8,0},{12,4},{16,24},{20,28},{24,16},{28,20},{1,9},{5... | collective-permute-start | bytes 393224 | tf_op jit(solution)/shard_map/ppermute | solution.py:26
  86.9 19.8 %collective-permute-start.25 = (bf16[128,512]{1,0:T(8,128)(2,1)S(1)}, bf16[128,512]{1,0:T(8,128)(2,1)S(1)}, u32[]{:S(2)}, u32[]{:S(2)}) collective-permute-start(bf16[128,512]{1,0:T(8,128)(2,1)S(1)} %shard_map.119.refs_0_), channel_id=1, source_target_pairs={{0,4},{4,0},{8,12},{12,8},{16,20},{20,16},{24,28},{28,24},{1,5},{5... | collective-permute-start | bytes 393224 | tf_op jit(solution)/shard_map/ppermute | solution.py:26
  95.8 10.9 %collective-permute-start.26 = (bf16[128,512]{1,0:T(8,128)(2,1)S(1)}, bf16[128,512]{1,0:T(8,128)(2,1)S(1)}, u32[]{:S(2)}, u32[]{:S(2)}) collective-permute-start(bf16[128,512]{1,0:T(8,128)(2,1)S(1)} %collective-permute-done.24.refs_1_), channel_id=1, source_target_pairs={{0,4},{4,0},{8,12},{12,8},{16,20},{20,16},{24,28},{28,24},{1,5},{5... | collective-permute-start | bytes 393224 | tf_op jit(solution)/shard_map/ppermute | solution.py:26
